TPU v7x, 32 devices: a whole 2x2x4 slice. The times are simulated.
32 devices in a mesh: row: 16 (over z, x, core), col: 2 (over y).
Axes of the slice: x: 2, y: 2, z: 4, core: 2. Of those that a mesh axis runs over, the one named last changes fastest.
Arguments:
- base_velocity: bfloat16 [3, 512, 256, 384], P(None, 'row', 'col'), may hold values from -6 to 6
- velocity_step: bfloat16 [3, 512, 256, 384], P(None, 'row', 'col'), may hold values from -6 to 6
- adjoint_velocity: bfloat16 [3, 512, 256, 384], P(None, 'row', 'col'), may hold values from -6 to 6
- increment_weight: float32 [1], replicated, may hold values from 0.3 to 0.9
- streamwise_first: bfloat16 [3, 128, 128], replicated, may hold values from -0.3125 to 0.3125
- streamwise_second: bfloat16 [3, 128, 128], replicated, may hold values from -0.3125 to 0.3125
- normal_first: bfloat16 [512, 512], replicated, may hold values from -0.25 to 0.25
- normal_second: bfloat16 [512, 512], replicated, may hold values from -0.25 to 0.25
- spanwise_first: bfloat16 [256, 256], replicated, may hold values from -0.375 to 0.375
- spanwise_second: bfloat16 [256, 256], replicated, may hold values from -0.375 to 0.375
- wall_profile: float32 [2, 512], P(None, 'row'), may hold values from 0.5 to 1.5
Outputs:
- adjoint_tendency: bfloat16 [3, 512, 256, 384], P(None, 'row', 'col')
All inputs are finite; a program needn't handle non-finite values.
Results may differ from a plain program's by a relative error of at most 0.012.
Values may be sent and summed in bfloat16 or wider, within the bound.
No kernel may reach another device: no remote copies, remote signals or barrier semaphores. Data moves between devices by JAX's collectives and lax.ppermute only.
A program may use at most 448 MiB of HBM per device.

v0:
```python
import jax
import jax.numpy as jnp
from jax import lax
from jax.sharding import PartitionSpec as P


def along_stream(field, operators):
    block_width = operators[0].shape[1]
    block_count = field.shape[-1] // block_width
    tiles = field.reshape(field.shape[:-1] + (block_count, block_width))
    joined = jnp.concatenate([blocks[k] for blocks in operators for k in range(3)], axis=1)
    product = jnp.dot(tiles, joined, preferred_element_type=jnp.float32)
    results = []
    for number in range(len(operators)):
        start = 3 * number * block_width
        lower = product[..., start : start + block_width]
        middle = product[..., start + block_width : start + 2 * block_width]
        upper = product[..., start + 2 * block_width : start + 3 * block_width]
        combined = jnp.roll(lower, 1, axis=-2) + middle + jnp.roll(upper, -1, axis=-2)
        results.append(combined.reshape(field.shape))
    return results


def normal_products(speed, adjoint, first_op, second_op):
    slope_speed = jnp.einsum("wy,cyp->cwp", first_op, speed, preferred_element_type=jnp.float32)
    stacked = jnp.concatenate([first_op, second_op], axis=0)
    both = jnp.einsum("wy,cyp->cwp", stacked, adjoint, preferred_element_type=jnp.float32)
    lines = first_op.shape[0]
    return (slope_speed, both[:, :lines], both[:, lines:])


def span_products(speed, adjoint, first_op, second_op):
    slope_speed = jnp.einsum("vz,cyzx->cyvx", first_op, speed, preferred_element_type=jnp.float32)
    stacked = jnp.concatenate([first_op, second_op], axis=0)
    both = jnp.einsum("vz,cyzx->cyvx", stacked, adjoint, preferred_element_type=jnp.float32)
    planes = first_op.shape[0]
    return (slope_speed, both[:, :, :planes], both[:, :, planes:])


def component_mask(which, ndim):
    return (jnp.arange(3) == which).astype(jnp.float32).reshape((3,) + (1,) * (ndim - 1))


def adjoint_terms(velocity, adjoint, slope_velocity, slope_adjoint, curve_adjoint, direction):
    cross = jnp.sum(adjoint.astype(jnp.float32) * slope_velocity, axis=0)
    advect = velocity[direction].astype(jnp.float32)[None] * slope_adjoint
    return curve_adjoint - advect + component_mask(direction, adjoint.ndim) * cross[None]


def per_device(
    base_velocity,
    velocity_step,
    adjoint_velocity,
    increment_weight,
    streamwise_first,
    streamwise_second,
    normal_first,
    normal_second,
    spanwise_first,
    spanwise_second,
    wall_profile,
):
    velocity = (
        base_velocity.astype(jnp.float32) + increment_weight[0] * velocity_step.astype(jnp.float32)
    ).astype(jnp.bfloat16)
    (slope_speed,) = along_stream(velocity, [streamwise_first])
    slope_adjoint, curve_adjoint = along_stream(
        adjoint_velocity, [streamwise_first, streamwise_second]
    )
    near = adjoint_terms(velocity, adjoint_velocity, slope_speed, slope_adjoint, curve_adjoint, 0)
    local_rows = velocity.shape[1]
    local_planes = velocity.shape[2]
    stream_cells = velocity.shape[3]
    flat_speed = velocity.reshape(3, local_rows, local_planes * stream_cells)
    flat_adjoint = adjoint_velocity.reshape(3, local_rows, local_planes * stream_cells)
    speed_lines, adjoint_lines = (
        lax.all_to_all(flat_speed, "row", split_axis=2, concat_axis=1, tiled=True),
        lax.all_to_all(flat_adjoint, "row", split_axis=2, concat_axis=1, tiled=True),
    )
    normal_speed, normal_adjoint, normal_curve = normal_products(
        speed_lines, adjoint_lines, normal_first, normal_second
    )
    normal_term = adjoint_terms(
        speed_lines, adjoint_lines, normal_speed, normal_adjoint, normal_curve, 1
    ).astype(jnp.bfloat16)
    strip = jnp.stack([normal_speed[0, 0], normal_speed[0, -1]]).astype(jnp.bfloat16)
    wall_shear = lax.all_gather(strip, "row", axis=1, tiled=True).reshape(
        2, local_planes, stream_cells
    )
    normal_home = lax.all_to_all(
        normal_term, "row", split_axis=1, concat_axis=2, tiled=True
    ).reshape(3, local_rows, local_planes, stream_cells)
    speed_span, adjoint_span = (
        lax.all_to_all(velocity, "col", split_axis=1, concat_axis=2, tiled=True),
        lax.all_to_all(adjoint_velocity, "col", split_axis=1, concat_axis=2, tiled=True),
    )
    span_speed, span_adjoint, span_curve = span_products(
        speed_span, adjoint_span, spanwise_first, spanwise_second
    )
    span_term = adjoint_terms(
        speed_span, adjoint_span, span_speed, span_adjoint, span_curve, 2
    ).astype(jnp.bfloat16)
    span_home = lax.all_to_all(span_term, "col", split_axis=2, concat_axis=1, tiled=True)
    far_terms = (normal_home.astype(jnp.float32) + span_home.astype(jnp.float32)).astype(
        jnp.bfloat16
    )
    (shear_slope,) = along_stream(wall_shear, [streamwise_first])
    forcing = (
        wall_profile[0][:, None, None] * shear_slope[0][None]
        + wall_profile[1][:, None, None] * shear_slope[1][None]
    )
    total = near + far_terms.astype(jnp.float32) + component_mask(0, 4) * forcing[None]
    return total.astype(jnp.bfloat16)


def solution(mesh):
    placed = (
        P(None, "row", "col", None),
        P(None, "row", "col", None),
        P(None, "row", "col", None),
        P(),
        P(),
        P(),
        P(),
        P(),
        P(),
        P(),
        P(None, "row"),
    )
    return jax.shard_map(
        per_device,
        mesh=mesh,
        in_specs=placed,
        out_specs=P(None, "row", "col", None),
        check_vma=False,
    )
```

profile of v0, /device:TPU:11, one launch (start us, length us, event | category | flops | bytes accessed | tf_op | source)
XLA Modules:
  0.0 1363.9 jit_solution(14723358383659704467)
XLA Ops:
  63.3 56.1 %all-to-all-done.3 = bf16[3,32,128,384]{3,2,0,1:T(8,128)(2,1)} async-done(((bf16[3,32,128,384]{3,2,0,1:T(8,128)(2,1)}), bf16[3,32,128,384]{3,2,0,1:T(8,128)(2,1)}, u32[]{:S(2)}, u32[]{:S(2)}) %all-to-all-start.3) | async-done | bytes 9437216 | tf_op jit(solution)/shard_map/all_to_all | solution.py:95
  126.8 81.2 %copy.232 = bf16[3,32,128,384]{1,0,3,2:T(4,128)(2,1)} copy(bf16[3,32,128,384]{2,3,1,0:T(8,128)(2,1)} %add_convert_fusion.2) | data formatting | bytes 18874368 | tf_op jit(solution)/shard_map/reshape | solution.py:74
  208.0 36.1 %reshape.104 = bf16[16,2,147456]{2,1,0:T(2,128)(2,1)} reshape(bf16[49152,3,32]{2,1,0:T(4,128)(2,1)} %bitcast.130) | data formatting | bytes 18874368
  251.5 48.7 %copy.195 = bf16[3,32,128,384]{1,0,3,2:T(4,128)(2,1)} copy(bf16[3,32,128,384]{3,2,1,0:T(8,128)(2,1)} %param.13) | data formatting | bytes 18874368 | tf_op args[2]
  300.2 36.1 %reshape.102 = bf16[16,2,147456]{2,1,0:T(2,128)(2,1)} reshape(bf16[49152,3,32]{2,1,0:T(4,128)(2,1)} %bitcast.131) | data formatting | bytes 18874368
  336.3 120.0 %all-to-all-done.1 = bf16[16,2,147456]{2,1,0:T(2,128)(2,1)} async-done(((bf16[16,2,147456]{2,1,0:T(2,128)(2,1)}), bf16[16,2,147456]{2,1,0:T(2,128)(2,1)}, u32[]{:S(2)}, u32[]{:S(2)}) %all-to-all-start.1) | async-done | bytes 9437216 | tf_op jit(solution)/shard_map/all_to_all | solution.py:77
  475.6 40.9 %convolution_bitcast_fusion = f32[3,32,128,3,768]{2,4,3,1,0:T(8,128)} fusion(bf16[3,32,128,3,128]{2,4,3,1,0:T(8,128)(2,1)} %bitcast.132, bf16[128,768]{0,1:T(8,128)(2,1)S(1)} %bitcast_dynamic-update-slice_fusion), kind=kOutput, calls=%fused_computation | convolution fusion | flops 7247757312 | bytes 122880000 | tf_op jit(solution)/shard_map/dot_general | solution.py:12
  516.5 31.5 %fusion.31 = (f32[3,32,128,2,128]{2,4,3,1,0:T(8,128)}, f32[3,32,128,2,128]{2,4,3,1,0:T(8,128)}, f32[3,32,128,2,128]{2,4,3,1,0:T(8,128)}, f32[3,32,128,2,128]{2,4,3,1,0:T(8,128)}) fusion(f32[3,32,128,3,768]{2,4,3,1,0:T(8,128)} %convolution_bitcast_fusion), kind=kLoop, calls=%fused_computation.69 | loop fusion | bytes 100663296 | tf_op jit(solution)/shard_map/jit(_roll_static)/slice | solution.py:19
  588.3 18.7 %convolution_bitcast_fusion.2 = f32[3,16,512,384]{3,2,1,0:T(8,128)} fusion(bf16[3,16,256,384]{3,2,1,0:T(8,128)(2,1)} %bitcast.134, bf16[256,256]{1,0:T(8,128)(2,1)S(1)} %copy-done.8, bf16[256,256]{1,0:T(8,128)(2,1)S(1)} %copy-done.1), kind=kOutput, calls=%fused_computation.28 | convolution fusion | flops 4832362496 | bytes 47448064 | tf_op jit(solution)/shard_map/vz,cyzx->cyvx/dot_general | solution.py:35
  607.0 19.0 %fusion.2 = bf16[3,16,256,384]{3,2,1,0:T(8,128)(2,1)} fusion(f32[3,16,512,384]{3,2,1,0:T(8,128)} %convolution_bitcast_fusion.2, f32[16,256,384]{2,1,0:T(8,128)} %fusion.9, f32[3]{0:T(128)S(1)} %compare_convert_fusion, f32[16,256,384]{2,1,0:T(8,128)S(1)} %bitcast.146), kind=kLoop, calls=%fused_computation.5 | loop fusion | flops 23592960 | bytes 59768844 | tf_op jit(solution)/shard_map/convert_element_type | solution.py:102
  638.8 35.8 %reshape.105 = bf16[49152,3,32]{2,1,0:T(4,128)(2,1)} reshape(bf16[16,2,147456]{2,1,0:T(2,128)(2,1)} %all-to-all-done.1) | data formatting | bytes 18874368
  674.6 58.5 %copy.234 = bf16[3,32,16,3072]{3,1,2,0:T(8,128)(2,1)} copy(bf16[3,32,16,3072]{1,0,3,2:T(4,128)(2,1)} %bitcast.126) | data formatting | bytes 18874368 | tf_op jit(solution)/shard_map/all_to_all | solution.py:77
  733.1 47.1 %copy.233 = bf16[3,32,16,3072]{3,2,1,0:T(8,128)(2,1)} copy(bf16[3,32,16,3072]{1,0,3,2:T(4,128)(2,1)} %bitcast.127) | data formatting | bytes 18874368 | tf_op jit(solution)/shard_map/all_to_all | solution.py:77
  787.7 36.2 %reshape.103 = bf16[49152,3,32]{2,1,0:T(4,128)(2,1)} reshape(bf16[16,2,147456]{2,1,0:T(2,128)(2,1)} %all-to-all-done) | data formatting | bytes 18874368
  823.9 58.5 %copy.231 = bf16[3,32,16,3072]{3,1,2,0:T(8,128)(2,1)} copy(bf16[3,32,16,3072]{1,0,3,2:T(4,128)(2,1)} %bitcast.129) | data formatting | bytes 18874368 | tf_op jit(solution)/shard_map/all_to_all | solution.py:78
  916.6 20.3 %convolution_bitcast_fusion.1 = f32[3,1024,3072]{2,1,0:T(8,128)} fusion(bf16[3,512,3072]{2,1,0:T(8,128)(2,1)} %bitcast.143, bf16[512,512]{1,0:T(8,128)(2,1)S(1)} %copy-done.13, bf16[512,512]{1,0:T(8,128)(2,1)S(1)} %copy-done), kind=kOutput, calls=%fused_computation.27 | convolution fusion | flops 9665773568 | bytes 48234496 | tf_op jit(solution)/shard_map/wy,cyp->cwp/dot_general | solution.py:27
  953.8 39.2 %copy.203 = bf16[3,512,3072]{2,0,1:T(4,128)(2,1)} copy(bf16[3,512,3072]{2,1,0:T(8,128)(2,1)S(1)} %fusion.5) | data formatting | bytes 18874368 | tf_op jit(solution)/shard_map/convert_element_type | solution.py:85
  1015.3 50.3 %fusion.7 = (f32[3,32,128,3,128]{2,4,3,1,0:T(8,128)}, f32[3,32,128,3,128]{2,4,3,1,0:T(8,128)}) fusion(f32[3,32,128,3,768]{2,4,3,1,0:T(8,128)} %convolution_bitcast_fusion, f32[3,32,128,2,128]{2,4,3,1,0:T(8,128)} %get-tuple-element.8, f32[3,32,128,1,128]{2,4,3,1,0:T(8,128)} %get-tuple-element.12, f32[3,32,128,1,128]{2,4,3,1,0:T(8,128)} %get-tuple-element.11, ...), kind=kLoop, calls=%fused_computation.13 | loop fusion | flops 37748736 | bytes 150994944 | tf_op jit(solution)/shard_map/add | solution.py:19
  1084.3 18.7 %copy.188 = f32[3,32,128,384]{3,2,1,0:T(8,128)} copy(f32[3,32,128,384]{2,3,1,0:T(8,128)} %bitcast.135) | data formatting | bytes 37748736 | tf_op jit(solution)/shard_map/reshape | solution.py:20
  1103.0 24.5 %fusion.25 = f32[3,32,128,3,384]{4,2,3,1,0:T(8,128)} fusion(bf16[3,32,128,3,128]{2,4,3,1,0:T(8,128)(2,1)} %bitcast.128, bf16[128,128]{0,1:T(8,128)(2,1)S(1)} %bitcast.155, bf16[128,128]{0,1:T(8,128)(2,1)S(1)} %bitcast.153, bf16[128,128]{0,1:T(8,128)(2,1)S(1)} %bitcast.151), kind=kOutput, calls=%fused_computation.49 | convolution fusion | flops 3624173568 | bytes 66158592 | tf_op jit(solution)/shard_map/dot_general | solution.py:12
  1150.9 19.5 %fusion.6 = f32[3,32,128,3,128]{4,2,3,1,0:T(8,128)} fusion(f32[3,32,128,3,384]{4,2,3,1,0:T(8,128)} %fusion.25, f32[3,32,128,2,128]{4,2,3,1,0:T(8,128)} %get-tuple-element.16, f32[3,32,128,1,128]{4,2,3,1,0:T(8,128)} %get-tuple-element.18, f32[3,32,128,1,128]{4,2,3,1,0:T(8,128)S(1)} %get-tuple-element.17, f32[3,32,128,2,128]{4,2,3,1,0:T(8,128)S(1)} %get-tuple-element.15), kind=kLoop, calls=%fused_computation.11 | loop fusion | flops 18874368 | bytes 75497472 | tf_op jit(solution)/shard_map/add | solution.py:19
  1249.2 32.3 %all_gather.3 = bf16[2,49152]{1,0:T(2,128)(2,1)S(1)} all-gather(bf16[2,3072]{1,0:T(2,128)(2,1)S(1)} %pad_maximum_fusion.3), channel_id=1, replica_groups=mesh['row'=16,'col'=2] {'row'}, dimensions={1}, use_global_device_ids=true | all-gather | bytes 208896 | tf_op jit(solution)/shard_map/all_gather | solution.py:87
  1308.4 20.5 %reshape.90 = f32[3,32,128,384]{3,2,1,0:T(8,128)} reshape(f32[3,32,16,3072]{3,2,1,0:T(8,128)} %copy.204) | data formatting | bytes 37748736 | tf_op jit(solution)/shard_map/convert_element_type | solution.py:104
  1328.9 34.6 %add_convert_fusion = bf16[3,32,128,384]{3,2,1,0:T(8,128)(2,1)} fusion(f32[3,32,128,384]{3,2,1,0:T(8,128)} %copy.189, f32[3,32,128,384]{3,2,1,0:T(8,128)} %copy.188, f32[3,32,128,384]{3,2,1,0:T(8,128)} %reshape.90, f32[3,32,128,384]{3,2,1,0:T(8,128)} %bitcast.137, f32[32,128,384]{2,1,0:T(8,128)} %multiply_add_fusion, f32[32,128,384]{2,1,0:T(8,128)} %copy.194, ...), kind=kLoop, calls=%fused_computation.24 | loop fusion | flops 51904512 | bytes 103809040 | tf_op jit(solution)/shard_map/convert_element_type | solution.py:113
  (111 shorter events, 378.2 us)
Async XLA Ops:
  9.1 110.3 %all-to-all-start.3 = ((bf16[3,32,128,384]{3,2,0,1:T(8,128)(2,1)}), bf16[3,32,128,384]{3,2,0,1:T(8,128)(2,1)}, u32[]{:S(2)}, u32[]{:S(2)}) async-start(bf16[3,32,128,384]{3,2,0,1:T(8,128)(2,1)} %copy.205), calls=%async_computation.3 | async-start | bytes 18874368 | tf_op jit(solution)/shard_map/all_to_all | solution.py:95
  119.4 124.6 %all-to-all-start.4 = ((bf16[3,32,128,384]{2,3,0,1:T(8,128)(2,1)}), bf16[3,32,128,384]{2,3,0,1:T(8,128)(2,1)}, u32[]{:S(2)}, u32[]{:S(2)}) async-start(bf16[3,32,128,384]{2,3,0,1:T(8,128)(2,1)} %copy.207), calls=%async_computation.4 | async-start | bytes 18874368 | tf_op jit(solution)/shard_map/all_to_all | solution.py:94
  244.1 212.2 %all-to-all-start.1 = ((bf16[16,2,147456]{2,1,0:T(2,128)(2,1)}), bf16[16,2,147456]{2,1,0:T(2,128)(2,1)}, u32[]{:S(2)}, u32[]{:S(2)}) async-start(bf16[16,2,147456]{2,1,0:T(2,128)(2,1)} %reshape.104), calls=%async_computation.1 | async-start | bytes 18874368 | tf_op jit(solution)/shard_map/all_to_all | solution.py:77
  456.3 323.9 %all-to-all-start = ((bf16[16,2,147456]{2,1,0:T(2,128)(2,1)}), bf16[16,2,147456]{2,1,0:T(2,128)(2,1)}, u32[]{:S(2)}, u32[]{:S(2)}) async-start(bf16[16,2,147456]{2,1,0:T(2,128)(2,1)} %reshape.102), calls=%async_computation | async-start | bytes 18874368 | tf_op jit(solution)/shard_map/all_to_all | solution.py:78
  461.5 12.7 copy-start.9
  461.5 13.1 copy-start.10
  474.4 42.2 %copy-start.2 = (bf16[1,128,128]{1,2,0:T(8,128)(2,1)}, bf16[1,128,128]{1,2,0:T(8,128)(2,1)S(1)}, u32[]{:S(2)}) copy-start(bf16[1,128,128]{1,2,0:T(8,128)(2,1)S(1)} %copy.239) | copy-start | bytes 98308
  474.5 42.1 %copy-start.4 = (bf16[1,128,128]{1,2,0:T(8,128)(2,1)}, bf16[1,128,128]{1,2,0:T(8,128)(2,1)S(1)}, u32[]{:S(2)}) copy-start(bf16[1,128,128]{1,2,0:T(8,128)(2,1)S(1)} %copy.240) | copy-start | bytes 98308
  474.6 41.9 %copy-start.6 = (bf16[1,128,128]{1,2,0:T(8,128)(2,1)}, bf16[1,128,128]{1,2,0:T(8,128)(2,1)S(1)}, u32[]{:S(2)}) copy-start(bf16[1,128,128]{1,2,0:T(8,128)(2,1)S(1)} %copy.241) | copy-start | bytes 98308
  575.5 12.7 copy-start.8
  575.5 31.4 %slice-start.3 = ((s8[6291456]{0:T(1024)(128)(4,1)}), s8[2097152]{0:T(1024)(128)(4,1)S(1)}, s32[]{:S(2)}) async-start(s8[6291456]{0:T(1024)(128)(4,1)} %bitcast.145), calls=%async_computation.9 | async-start | bytes 4194304
  588.3 18.7 %slice-start.4 = ((s8[6291456]{0:T(1024)(128)(4,1)}), s8[4194304]{0:T(1024)(128)(4,1)S(1)}, s32[]{:S(2)}) async-start(s8[6291456]{0:T(1024)(128)(4,1)} %bitcast.145), calls=%async_computation.10 | async-start | bytes 8388608
  780.2 212.7 %all-to-all-start.5 = ((bf16[3,16,256,384]{3,1,0,2:T(8,128)(2,1)}), bf16[3,16,256,384]{3,1,0,2:T(8,128)(2,1)}, u32[]{:S(2)}, u32[]{:S(2)}) async-start(bf16[3,16,256,384]{3,1,0,2:T(8,128)(2,1)} %copy.212), calls=%async_computation.5 | async-start | bytes 18874368 | tf_op jit(solution)/shard_map/all_to_all | solution.py:103
  882.4 9.2 slice-start
  882.4 9.2 copy-start
  882.4 9.2 slice-start.1
  885.2 6.3 slice-start.2
  903.5 13.1 copy-start.13
  916.6 20.3 %copy-start.12 = (f32[3]{0:T(128)S(1)}, f32[3]{0:T(128)}, u32[]{:S(2)}) copy-start(f32[3]{0:T(128)} %compare_convert_fusion.1) | copy-start | bytes 40
  993.0 293.4 %all-to-all-start.2 = ((bf16[3,512,3072]{2,0,1:T(4,128)(2,1)}), bf16[3,512,3072]{2,0,1:T(4,128)(2,1)}, u32[]{:S(2)}, u32[]{:S(2)}) async-start(bf16[3,512,3072]{2,0,1:T(4,128)(2,1)} %copy.203), calls=%async_computation.2 | async-start | bytes 25165824 | tf_op jit(solution)/shard_map/all_to_all | solution.py:90
  1084.3 18.7 %copy-start.3 = (bf16[1,128,128]{1,2,0:T(8,128)(2,1)S(1)}, bf16[1,128,128]{1,2,0:T(8,128)(2,1)}, u32[]{:S(2)}) copy-start(bf16[1,128,128]{1,2,0:T(8,128)(2,1)} %copy-done.2) | copy-start | bytes 98308
  1084.3 18.7 %copy-start.5 = (bf16[1,128,128]{1,2,0:T(8,128)(2,1)S(1)}, bf16[1,128,128]{1,2,0:T(8,128)(2,1)}, u32[]{:S(2)}) copy-start(bf16[1,128,128]{1,2,0:T(8,128)(2,1)} %copy-done.4) | copy-start | bytes 98308
  1084.3 18.7 %copy-start.7 = (bf16[1,128,128]{1,2,0:T(8,128)(2,1)S(1)}, bf16[1,128,128]{1,2,0:T(8,128)(2,1)}, u32[]{:S(2)}) copy-start(bf16[1,128,128]{1,2,0:T(8,128)(2,1)} %copy-done.6) | copy-start | bytes 98308
  1209.0 11.9 copy-start.11
  (1 other events, 5.7 us)
where the time goes:
time: 1380 us; the launch traced here: 1360 us
  local copies, waits for them, and re-layouts  768 us (56%)
  other arithmetic  215 us (16%)
  waiting for transfers between devices  176 us (13%)
  matrix products  129 us (9%)
  starting transfers between devices  41.1 us (3%)
  blocking collectives  32.3 us (2%)
    unnamed x58, local copies, waits for them, and re-layouts  241 us
    all_to_all x1, waiting for transfers between devices, per_device(): lax.all_to_all(flat_speed, 'row', split_axis=2, concat_axis=1, tiled=True)  120 us
    all_to_all x2, local copies, waits for them, and re-layouts, per_device(): lax.all_to_all(flat_speed, 'row', split_axis=2, concat_axis=1, tiled=True)  106 us
    reshape x1, local copies, waits for them, and re-layouts, per_device(): flat_speed = velocity.reshape(3, local_rows, local_planes * stream_cells)  81.2 us
    slice x6, local copies, waits for them, and re-layouts, along_stream(): jnp.roll(upper, -1, axis=-2)  71 us
    add x3, other arithmetic, along_stream(): jnp.roll(lower, 1, axis=-2) + middle + jnp.roll(upper, -1, axis=-2)  69.8 us
    dot_general x3, matrix products, along_stream(): product = jnp.dot(tiles, joined, preferred_element_type=jnp.float32)  65.7 us
    all_to_all x1, local copies, waits for them, and re-layouts, per_device(): lax.all_to_all(flat_adjoint, 'row', split_axis=2, concat_axis=1, tiled=True)  58.5 us
  transfers between devices with their start and end apart: 6, of which 2 were waited for; matrix products, arithmetic and copies ran while one was open for 75% of the time, Pallas kernels for 0%

commit v1 on v0

v1 whole, which is shorter than its diff:
```python
import functools

import jax
import jax.numpy as jnp
from jax import lax
from jax.experimental import pallas as pl
from jax.experimental.pallas import tpu as pltpu
from jax.sharding import PartitionSpec as P

F32 = jnp.float32
BF16 = jnp.bfloat16
LANES = 128
VMEM_LIMIT = 56 * 1024 * 1024


def params():
    return pltpu.CompilerParams(vmem_limit_bytes=VMEM_LIMIT)


def cost(flops, bytes_accessed):
    return pl.CostEstimate(flops=flops, bytes_accessed=bytes_accessed, transcendentals=0)


def resident(shape):
    return pl.BlockSpec(shape, lambda *_: (0,) * len(shape))


def unread():
    return pl.BlockSpec(memory_space=pl.ANY)


def mixed(weight, base, step):
    return (base.astype(F32) + weight * step.astype(F32)).astype(BF16)


def prepare_kernel(weight_ref, base_ref, step_ref, adjoint_ref, *refs):
    sent_ref, turned = refs[-2:]
    rows, planes, cells = base_ref.shape[1:]
    weight = weight_ref[0]
    for part in range(cells // LANES):
        lanes = pl.ds(part * LANES, LANES)
        for field in range(6):
            component = field % 3
            if field < 3:
                value = mixed(weight, base_ref[component, :, :, lanes], step_ref[component, :, :, lanes])
                value = value.astype(F32)
            else:
                value = adjoint_ref[component, :, :, lanes].astype(F32)
            turned[field % 2] = value.reshape(rows * planes, LANES)
            for plane in range(planes):
                sent_ref[plane, field, :, lanes] = turned[
                    field % 2, pl.ds(plane, rows, stride=planes), :
                ].astype(BF16)


def prepare(weight, base, step, adjoint, earlier, first, count, width):
    _, rows, _, cells = base.shape
    start = first // width
    source = pl.BlockSpec((3, rows, width, cells), lambda i: (0, 0, start + i, 0))
    scalars = pl.BlockSpec(memory_space=pltpu.SMEM)
    return pl.pallas_call(
        prepare_kernel,
        grid=(count // width,),
        in_specs=[scalars, source, source, source] + [unread()] * len(earlier),
        out_specs=pl.BlockSpec((width, 6, rows, cells), lambda i: (i, 0, 0, 0)),
        out_shape=jax.ShapeDtypeStruct((count, 6, rows, cells), BF16),
        scratch_shapes=[pltpu.VMEM((2, rows * width, LANES), F32)],
        compiler_params=params(),
        cost_estimate=cost(0, 30 * count * rows * cells),
        name="prepare",
    )(weight, base, step, adjoint, *earlier)


def strip_rows(planes):
    return next(total for total in range(8, 16 * planes + 8, 8) if total % planes == 0 and total >= 2 * planes)


def normal_kernel(planes, first_ref, second_ref, lines_ref, *refs):
    out_ref, strips = refs[-2:]
    owners, _, _, rows, cells = lines_ref.shape
    lines = owners * rows
    plane = pl.program_id(0)

    def whole(field):
        return lines_ref[:, 0, field].reshape(lines, cells)

    @pl.when(plane == 0)
    def _():
        strips[...] = jnp.zeros_like(strips)

    first = first_ref[...]
    second = second_ref[...]
    cross = None
    for component in range(3):
        slope = jnp.dot(first, whole(component), preferred_element_type=F32)
        if component == 0:
            place = plane * (strips.shape[0] // planes)
            strips[pl.ds(place, 1), :] = slope[:1]
            strips[pl.ds(place + 1, 1), :] = slope[lines - 1 :]
        term = whole(3 + component).astype(F32) * slope
        cross = term if cross is None else cross + term
    speed = whole(1).astype(F32)
    for component in range(3):
        field = whole(3 + component)
        slope = jnp.dot(first, field, preferred_element_type=F32)
        term = jnp.dot(second, field, preferred_element_type=F32) - speed * slope
        if component == 1:
            term = term + cross
        place = pl.multiple_of((3 * plane + component) * rows, rows)
        out_ref[:, pl.ds(place, rows), :] = term.astype(BF16).reshape(owners, rows, cells)

    @pl.when(plane == planes - 1)
    def _():
        last = strips[...].astype(BF16)
        for owner in range(owners):
            out_ref[owner, 3 * planes * rows :, :] = last


def normal(first_op, second_op, received, earlier):
    owners, planes, _, rows, cells = received.shape
    lines = owners * rows
    length = 3 * planes * rows + strip_rows(planes)
    return pl.pallas_call(
        functools.partial(normal_kernel, planes),
        grid=(planes,),
        in_specs=[
            resident((lines, lines)),
            resident((lines, lines)),
            pl.BlockSpec((owners, 1, 6, rows, cells), lambda p: (0, p, 0, 0, 0)),
        ]
        + [unread()] * len(earlier),
        out_specs=resident((owners, length, cells)),
        out_shape=jax.ShapeDtypeStruct((owners, length, cells), BF16),
        scratch_shapes=[pltpu.VMEM((strip_rows(planes), cells), F32)],
        compiler_params=params(),
        cost_estimate=cost(18 * planes * lines * lines * cells, 18 * planes * lines * cells),
        name="normal",
    )(first_op, second_op, received, *earlier)


def near_kernel(parts, weight_ref, stream_ref, curve_ref, cross_ref, base_ref, step_ref, *refs):
    adjoint_refs = refs[:parts]
    near_ref = refs[-parts]
    partial_refs = refs[len(refs) - parts + 1 :]
    _, _, planes, cells = base_ref.shape
    weight = weight_ref[0]
    stream = stream_ref[...]
    curve = curve_ref[...]
    speeds = [mixed(weight, base_ref[c, 0], step_ref[c, 0]) for c in range(3)]
    adjoints = [[ref[c, 0] for ref in adjoint_refs] for c in range(3)]
    stream_cross = None
    span_cross = [None] * parts
    for c in range(3):
        slope = jnp.dot(speeds[c], stream[:, :cells], preferred_element_type=F32)
        term = adjoints[c][0].astype(F32) * slope
        stream_cross = term if stream_cross is None else stream_cross + term
        slopes = jnp.dot(cross_ref[...], speeds[c], preferred_element_type=F32)
        for part in range(parts):
            term = adjoints[c][part].astype(F32) * slopes[part * planes : (part + 1) * planes]
            span_cross[part] = term if span_cross[part] is None else span_cross[part] + term
    for part in range(1, parts):
        partial_refs[part - 1][0] = span_cross[part].astype(BF16)
    for c in range(3):
        along = jnp.dot(adjoints[c][0], stream, preferred_element_type=F32)
        total = along[:, cells:] - speeds[0].astype(F32) * along[:, :cells]
        across = jnp.dot(curve, jnp.concatenate(adjoints[c], axis=0), preferred_element_type=F32)
        total += across[planes:] - speeds[2].astype(F32) * across[:planes]
        if c == 0:
            total += stream_cross
        if c == 2:
            total += span_cross[0]
        near_ref[c, 0] = total.astype(BF16)


def near(weight, stream, curve, cross, base, step, own, others, previous, first):
    _, rows, planes, cells = base.shape
    parts = 1 + len(others)
    count = rows if not others else others[0].shape[1]
    row_of = pl.BlockSpec((3, 1, planes, cells), lambda i: (0, first + i, 0, 0))
    row_one = pl.BlockSpec((1, planes, cells), lambda i: (first + i, 0, 0))
    scalars = pl.BlockSpec(memory_space=pltpu.SMEM)
    operands = [weight, stream, curve, cross, base, step, own, *others]
    aliases = {}
    if previous is not None:
        aliases = {len(operands) + k: k for k in range(parts)}
        operands += previous
    return pl.pallas_call(
        functools.partial(near_kernel, parts),
        grid=(count,),
        in_specs=[scalars]
        + [resident(operand.shape) for operand in operands[1:4]]
        + [row_of] * 3
        + [pl.BlockSpec((3, 1, planes, cells), lambda i: (0, i, 0, 0))] * (parts - 1)
        + [unread()] * len(aliases),
        out_specs=[row_of] + [row_one] * (parts - 1),
        out_shape=[jax.ShapeDtypeStruct(base.shape, BF16)]
        + [jax.ShapeDtypeStruct((rows, planes, cells), BF16)] * (parts - 1),
        input_output_aliases=aliases,
        compiler_params=params(),
        cost_estimate=cost(
            18 * count * planes * cells * (cells + parts * planes), 6 * count * planes * cells * (4 + parts)
        ),
        name="near",
    )(*operands)


def finish_kernel(partials, planes, profile_ref, stream_ref, home_ref, near_ref, *refs):
    partial_refs = refs[:partials]
    out_ref, turned, strips, slopes = refs[-4:]
    owners, length, cells = home_ref.shape
    rows = out_ref.shape[1]
    width = owners * planes
    held = length - 3 * planes * rows
    pitch = held // planes
    for owner in range(owners):
        strips[owner * held : (owner + 1) * held, :] = home_ref[owner, 3 * planes * rows :, :].astype(F32)
    slope = jnp.dot(strips[...].astype(BF16), stream_ref[...], preferred_element_type=F32)
    for part in range(cells // LANES):
        lanes = pl.ds(part * LANES, LANES)
        slopes[...] = slope[:, part * LANES : (part + 1) * LANES]
        lower = slopes[pl.ds(0, width, stride=pitch), :]
        upper = slopes[pl.ds(1, width, stride=pitch), :]
        for component in range(3):
            slot = component % 2
            for plane in range(width):
                place = (3 * (plane % planes) + component) * rows
                turned[slot, plane * rows : (plane + 1) * rows, :] = home_ref[
                    plane // planes, place : place + rows, lanes
                ].astype(F32)
            for row in range(rows):
                total = turned[slot, pl.ds(row, width, stride=rows), :]
                total += near_ref[component, row, :, lanes].astype(F32)
                if component == 0:
                    total += profile_ref[0, row] * lower + profile_ref[1, row] * upper
                if component == 2:
                    for ref in partial_refs:
                        total += ref[row, :, lanes].astype(F32)
                out_ref[component, row, :, lanes] = total.astype(BF16)


def finish(profile, stream, home, near_term, partials, previous, first, planes, width):
    owners, length, cells = home.shape
    rows = near_term.shape[1]
    start = first // width
    held = width // planes
    field = pl.BlockSpec((3, rows, width, cells), lambda i: (0, 0, start + i, 0))
    single = pl.BlockSpec((rows, width, cells), lambda i: (0, start + i, 0))
    operands = [profile, stream, home, near_term, *partials]
    specs = [
        pl.BlockSpec(memory_space=pltpu.SMEM),
        resident(stream.shape),
        pl.BlockSpec((held, length, cells), lambda i: (i, 0, 0)),
        field,
    ] + [single] * len(partials)
    aliases = {}
    if previous is not None:
        aliases = {len(operands): 0}
        operands.append(previous)
        specs.append(unread())
    return pl.pallas_call(
        functools.partial(finish_kernel, len(partials), planes),
        grid=(owners * planes // width,),
        in_specs=specs,
        out_specs=field,
        out_shape=jax.ShapeDtypeStruct(near_term.shape, BF16),
        scratch_shapes=[
            pltpu.VMEM((2, rows * width, LANES), F32),
            pltpu.VMEM((held * strip_rows(planes), cells), F32),
            pltpu.VMEM((held * strip_rows(planes), LANES), F32),
        ],
        input_output_aliases=aliases,
        compiler_params=params(),
        cost_estimate=cost(0, 22 * owners * planes * rows * cells),
        name="finish",
    )(*operands)


def joined_blocks(blocks, cells):
    count = cells // blocks.shape[1]
    columns = []
    for column in range(count):
        rows = [jnp.zeros(blocks.shape[1:], blocks.dtype)] * count
        for k in range(3):
            rows[(column + k - 1) % count] = rows[(column + k - 1) % count] + blocks[k]
        columns.append(jnp.concatenate(rows, axis=0))
    return jnp.concatenate(columns, axis=1)


def divide(planes):
    if planes < 2:
        return [planes]
    return [planes - planes // 2, planes // 2]


def per_device(
    base_velocity,
    velocity_step,
    adjoint_velocity,
    increment_weight,
    streamwise_first,
    streamwise_second,
    normal_first,
    normal_second,
    spanwise_first,
    spanwise_second,
    wall_profile,
):
    _, rows, planes, cells = base_velocity.shape
    owners = normal_first.shape[0] // rows
    parts = spanwise_first.shape[0] // planes
    width = 16
    slab = lax.axis_index("col")

    def from_others(start, count):
        piece = lax.slice_in_dim(adjoint_velocity, start, start + count, axis=1)
        return [
            lax.ppermute(piece, "col", [((i + shift) % parts, i) for i in range(parts)])
            for shift in range(1, parts)
        ]

    half = rows // 2
    others = [from_others(0, half), from_others(half, half)]

    chunks = divide(planes // owners)
    starts = [owners * sum(chunks[:k]) for k in range(len(chunks))]
    sent = []
    for chunk, start in zip(chunks, starts):
        block = prepare(
            increment_weight,
            base_velocity,
            velocity_step,
            adjoint_velocity,
            others[0] if sent else [],
            start,
            owners * chunk,
            width,
        )
        sent.append(block.reshape(owners, chunk, 6, rows, cells))

    received = [lax.all_to_all(block, "row", 0, 0, tiled=True) for block in sent]

    stream_first = joined_blocks(streamwise_first, cells)
    stream_second = joined_blocks(streamwise_second, cells)
    stream = jnp.concatenate([stream_first, stream_second], axis=1)

    def own_first(operator):
        return lax.dynamic_slice_in_dim(operator, slab * planes, planes, 0)

    def turned(operator, axis):
        return jnp.roll(operator, -slab * planes, axis=axis)

    curve = turned(jnp.concatenate([own_first(spanwise_first), own_first(spanwise_second)], axis=0), 1)
    cross = turned(lax.dynamic_slice_in_dim(spanwise_first, slab * planes, planes, 1), 0)
    local = None
    for number, pieces in enumerate(others):
        local = near(
            increment_weight,
            stream,
            curve,
            cross,
            base_velocity,
            velocity_step,
            adjoint_velocity,
            pieces,
            local,
            number * half,
        )
    near_term, *partials = local
    partials = [
        lax.ppermute(partial, "col", [(i, (i + shift) % parts) for i in range(parts)])
        for shift, partial in enumerate(partials, 1)
    ]

    returned = []
    for number, block in enumerate(received):
        earlier = others[1] if number == 0 else [near_term]
        term = normal(normal_first, normal_second, block, earlier)
        returned.append(lax.all_to_all(term, "row", 0, 0, tiled=True))
    result = None
    for block, start, chunk in zip(returned, starts, chunks):
        result = finish(
            wall_profile, stream_first, block, near_term, partials, result, start, chunk, width
        )
    return result


def solution(mesh):
    placed = (
        P(None, "row", "col", None),
        P(None, "row", "col", None),
        P(None, "row", "col", None),
        P(),
        P(),
        P(),
        P(),
        P(),
        P(),
        P(),
        P(None, "row"),
    )
    return jax.shard_map(
        per_device,
        mesh=mesh,
        in_specs=placed,
        out_specs=P(None, "row", "col", None),
        check_vma=False,
    )
```

time: 1380 us -> 668 us (0.48); the launches traced: 1360 us -> 667 us
  local copies, waits for them, and re-layouts: 768 us -> 15.3 us
  waiting for transfers between devices: 176 us -> 503 us
  other arithmetic: 215 us -> 2.91 us
  matrix products: 129 us -> 0 us
  Pallas kernels: 0 us -> 120 us
  blocking collectives: 32.3 us -> 0 us
  starting transfers between devices: 41.1 us -> 25.1 us
    ppermute x0 -> x3, waiting for transfers between devices: none -> 272 us  [the longest x2 204 us: from_others(): lax.ppermute(piece, 'col', [((i + shift) % parts, i) for i in range(parts)])]
    unnamed x58 -> x18, local copies, waits for them, and re-layouts: 241 us -> 5.94 us
    all_to_all x5 -> x0, local copies, waits for them, and re-layouts: 186 us -> none  [the longest x2 106 us: per_device(): lax.all_to_all(flat_speed, 'row', split_axis=2, concat_axis=1, tiled=True)]
    dot_general x7 -> x0, matrix products: 129 us -> none  [the longest x3 65.7 us: along_stream(): product = jnp.dot(tiles, joined, preferred_element_type=jnp.float32)]
    pallas_call x0 -> x8, Pallas kernels: none -> 120 us  [the longest x2 43.4 us: near(): pl.pallas_call(functools.partial(near_kernel, parts), grid=(count,), in_s...]
    reshape x3 -> x0, local copies, waits for them, and re-layouts: 119 us -> none  [the longest x1 81.2 us: per_device(): flat_speed = velocity.reshape(3, local_rows, local_planes * stream_cells)]
    convert_element_type x7 -> x0, local copies, waits for them, and re-layouts: 116 us -> none  [the longest x1 39.2 us: per_device(): normal_term = adjoint_terms(speed_lines, adjoint_lines, normal_speed, nor...]
    convert_element_type x11 -> x0, other arithmetic: 110 us -> none  [the longest x1 34.6 us: per_device(): return total.astype(jnp.bfloat16)]
  transfers between devices with their start and end apart: 6 -> 7, of which waited for: 2 -> 7; matrix products, arithmetic and copies ran while one was open for 75% -> 2% of each run, Pallas kernels for 0% -> 14%
where the time goes in v1:
time: 668 us; the launch traced here: 667 us
  waiting for transfers between devices  503 us (75%)
  Pallas kernels  120 us (18%)
  starting transfers between devices  25.1 us (4%)
  local copies, waits for them, and re-layouts  15.3 us (2%)
    ppermute x2, waiting for transfers between devices, from_others(): lax.ppermute(piece, 'col', [((i + shift) % parts, i) for i in range(parts)])  204 us
    all_to_all x2, waiting for transfers between devices, per_device(): lax.all_to_all(block, 'row', 0, 0, tiled=True)  161 us
    all_to_all x2, waiting for transfers between devices, per_device(): returned.append(lax.all_to_all(term, 'row', 0, 0, tiled=True))  69.8 us
    ppermute x1, waiting for transfers between devices, per_device(): lax.ppermute(partial, 'col', [(i, (i + shift) % parts) for i in range(par...  67.4 us
    pallas_call x2, Pallas kernels, near(): pl.pallas_call(functools.partial(near_kernel, parts), grid=(count,), in_s...  43.4 us
    pallas_call x2, Pallas kernels, normal(): pl.pallas_call(functools.partial(normal_kernel, planes), grid=(planes,),...  29.4 us
    pallas_call x2, Pallas kernels, prepare(): pl.pallas_call(prepare_kernel, grid=(count // width,), in_specs=[scalars,...  26.5 us
    pallas_call x2, Pallas kernels, finish(): pl.pallas_call(functools.partial(finish_kernel, len(partials), planes), g...  20.5 us
  transfers between devices with their start and end apart: 7, of which 7 were waited for; matrix products, arithmetic and copies ran while one was open for 2% of the time, Pallas kernels for 14%

profile of v1, /device:TPU:11, one launch (start us, length us, event | category | flops | bytes accessed | tf_op | source)
XLA Modules:
  0.0 666.7 jit_solution(15188260551335594140)
XLA Ops:
  0.7 13.3 %prepare.3 = bf16[64,6,32,384]{3,2,1,0:T(8,128)(2,1)} custom-call(f32[1]{0:T(128)S(6)} %copy.23.weight_ref, bf16[3,32,128,384]{3,2,1,0:T(8,128)(2,1)} %base_ref.7, bf16[3,32,128,384]{3,2,1,0:T(8,128)(2,1)} %step_ref.7, bf16[3,32,128,384]{3,2,1,0:T(8,128)(2,1)} %adjoint_ref.3), custom_call_target="tpu_custom_call" | custom-call | bytes 23592960 | tf_op jit(solution)/shard_map/prepare/pallas_call | solution.py:61
  13.9 6.6 all-to-all-start.2
  20.5 9.3 %fusion.4 = (bf16[3,16,128,384]{3,2,1,0:T(8,128)(2,1)}, bf16[3,16,128,384]{3,2,1,0:T(8,128)(2,1)}) fusion(bf16[3,32,128,384]{3,2,1,0:T(8,128)(2,1)} %adjoint_ref.3), kind=kLoop, calls=%fused_computation.26 | loop fusion | bytes 18874368 | tf_op jit(solution)/shard_map/slice | solution.py:315
  31.1 102.1 %collective-permute-done.refs_0_.refs_1_ = bf16[3,16,128,384]{3,2,1,0:T(8,128)(2,1)S(1)} collective-permute-done((bf16[3,16,128,384]{3,2,1,0:T(8,128)(2,1)}, bf16[3,16,128,384]{3,2,1,0:T(8,128)(2,1)S(1)}, u32[]{:S(2)}, u32[]{:S(2)}) %collective-permute-start) | collective-permute-done | bytes 4718624 | tf_op jit(solution)/shard_map/ppermute | solution.py:317
  133.2 2.1 copy-done
  135.3 13.2 %prepare.2 = bf16[64,6,32,384]{3,2,1,0:T(8,128)(2,1)} custom-call(f32[1]{0:T(128)S(6)} %copy.23.weight_ref, bf16[3,32,128,384]{3,2,1,0:T(8,128)(2,1)} %base_ref.7, bf16[3,32,128,384]{3,2,1,0:T(8,128)(2,1)} %step_ref.7, bf16[3,32,128,384]{3,2,1,0:T(8,128)(2,1)} %adjoint_ref.3, bf16[3,16,128,384]{3,2,1,0:T(8,128)(2,1)} %copy-done), custom_call_target="tpu_custom_call" | custom-call | bytes 23592960 | tf_op jit(solution)/shard_map/prepare/pallas_call | solution.py:61
  148.4 76.9 %all-to-all-done.2.lines_ref = bf16[16,4,6,32,384]{4,3,2,1,0:T(8,128)(2,1)} async-done(((bf16[16,4,6,32,384]{4,3,2,1,0:T(8,128)(2,1)}), bf16[16,4,6,32,384]{4,3,2,1,0:T(8,128)(2,1)}, u32[]{:S(2)}, u32[]{:S(2)}) %all-to-all-start.2) | async-done | bytes 9437216 | tf_op jit(solution)/shard_map/all_to_all | solution.py:340
  225.3 4.9 all-to-all-start
  231.5 102.0 %collective-permute-done.1.refs_1_.refs_0_ = bf16[3,16,128,384]{3,2,1,0:T(8,128)(2,1)S(1)} collective-permute-done((bf16[3,16,128,384]{3,2,1,0:T(8,128)(2,1)}, bf16[3,16,128,384]{3,2,1,0:T(8,128)(2,1)S(1)}, u32[]{:S(2)}, u32[]{:S(2)}) %collective-permute-start.1) | collective-permute-done | bytes 4718624 | tf_op jit(solution)/shard_map/ppermute | solution.py:317
  333.5 2.2 copy-done.2
  335.7 14.7 %normal.3 = bf16[16,392,384]{2,1,0:T(8,128)(2,1)} custom-call(bf16[512,512]{1,0:T(8,128)(2,1)} %first_ref.3, bf16[512,512]{1,0:T(8,128)(2,1)} %second_ref.3, bf16[16,4,6,32,384]{4,3,2,1,0:T(8,128)(2,1)} %all-to-all-done.2.lines_ref, bf16[3,16,128,384]{3,2,1,0:T(8,128)(2,1)} %copy-done.2), custom_call_target="tpu_custom_call" | custom-call | flops 7247757312 | bytes 14155776 | tf_op jit(solution)/shard_map/normal/pallas_call | solution.py:123
  350.4 84.6 %all-to-all-done.lines_ref = bf16[16,4,6,32,384]{4,3,2,1,0:T(8,128)(2,1)} async-done(((bf16[16,4,6,32,384]{4,3,2,1,0:T(8,128)(2,1)}), bf16[16,4,6,32,384]{4,3,2,1,0:T(8,128)(2,1)}, u32[]{:S(2)}, u32[]{:S(2)}) %all-to-all-start) | async-done | bytes 9437216 | tf_op jit(solution)/shard_map/all_to_all | solution.py:340
  435.0 4.9 all-to-all-start.3
  442.3 21.7 %near.2 = (bf16[3,32,128,384]{3,2,1,0:T(8,128)(2,1)}, bf16[32,128,384]{2,1,0:T(8,128)(2,1)}) custom-call(f32[1]{0:T(128)S(6)} %copy.23.weight_ref, bf16[384,768]{1,0:T(8,128)(2,1)} %copy-done.4, bf16[256,256]{1,0:T(8,128)(2,1)} %fusion.1.curve_ref, bf16[256,128]{1,0:T(8,128)(2,1)} %fusion.3.cross_ref, bf16[3,32,128,384]{3,2,1,0:T(8,128)(2,1)} %base_ref.7, ...), custom_call_target="tpu_custom_call" | custom-call | flops 9059696640 | bytes 28311552 | tf_op jit(solution)/shard_map/near/pallas_call | solution.py:187
  464.0 21.7 %near.3 = (bf16[3,32,128,384]{3,2,1,0:T(8,128)(2,1)}, bf16[32,128,384]{2,1,0:T(8,128)(2,1)}) custom-call(f32[1]{0:T(128)S(6)} %copy.23.weight_ref, bf16[384,768]{1,0:T(8,128)(2,1)} %copy-done.4, bf16[256,256]{1,0:T(8,128)(2,1)} %fusion.1.curve_ref, bf16[256,128]{1,0:T(8,128)(2,1)} %fusion.3.cross_ref, ...), custom_call_target="tpu_custom_call", output_to_operand_aliasing={{0}: (8, {}), {1}: (9, {})} | custom-call | flops 9059696640 | bytes 28311552 | tf_op jit(solution)/shard_map/near/pallas_call | solution.py:187
  485.7 14.6 %normal.2 = bf16[16,392,384]{2,1,0:T(8,128)(2,1)} custom-call(bf16[512,512]{1,0:T(8,128)(2,1)} %first_ref.3, bf16[512,512]{1,0:T(8,128)(2,1)} %second_ref.3, bf16[16,4,6,32,384]{4,3,2,1,0:T(8,128)(2,1)} %all-to-all-done.lines_ref, bf16[3,32,128,384]{3,2,1,0:T(8,128)(2,1)} %get-tuple-element.11.refs_0_.near_ref), custom_call_target="tpu_custom_call" | custom-call | flops 7247757312 | bytes 14155776 | tf_op jit(solution)/shard_map/normal/pallas_call | solution.py:123
  500.4 45.4 %all-to-all-done.3.home_ref = bf16[16,392,384]{2,1,0:T(8,128)(2,1)} async-done(((bf16[16,392,384]{2,1,0:T(8,128)(2,1)}), bf16[16,392,384]{2,1,0:T(8,128)(2,1)}, u32[]{:S(2)}, u32[]{:S(2)}) %all-to-all-start.3) | async-done | bytes 4816928 | tf_op jit(solution)/shard_map/all_to_all | solution.py:378
  545.8 4.9 all-to-all-start.1
  550.7 1.3 collective-permute-start.2
  552.7 67.4 %collective-permute-done.2.refs_0_ = bf16[32,128,384]{2,1,0:T(8,128)(2,1)S(1)} collective-permute-done((bf16[32,128,384]{2,1,0:T(8,128)(2,1)S(1)}, bf16[32,128,384]{2,1,0:T(8,128)(2,1)S(1)}, u32[]{:S(2)}, u32[]{:S(2)}) %collective-permute-start.2) | collective-permute-done | bytes 3145760 | tf_op jit(solution)/shard_map/ppermute | solution.py:370
  620.2 1.6 copy-done.1
  621.8 10.3 %finish.2.refs_1_ = bf16[3,32,128,384]{3,2,1,0:T(8,128)(2,1)} custom-call(f32[2,32]{1,0:T(2,128)} %profile_ref.3, bf16[384,384]{1,0:T(8,128)(2,1)} %maximum_maximum_fusion.stream_ref, bf16[16,392,384]{2,1,0:T(8,128)(2,1)} %all-to-all-done.3.home_ref, bf16[3,32,128,384]{3,2,1,0:T(8,128)(2,1)} %get-tuple-element.11.refs_0_.near_ref, ...), custom_call_target="tpu_custom_call" | custom-call | bytes 17301504 | tf_op jit(solution)/shard_map/finish/pallas_call | solution.py:260
  632.1 24.4 %all-to-all-done.1.home_ref = bf16[16,392,384]{2,1,0:T(8,128)(2,1)} async-done(((bf16[16,392,384]{2,1,0:T(8,128)(2,1)}), bf16[16,392,384]{2,1,0:T(8,128)(2,1)}, u32[]{:S(2)}, u32[]{:S(2)}) %all-to-all-start.1) | async-done | bytes 4816928 | tf_op jit(solution)/shard_map/all_to_all | solution.py:378
  656.5 10.3 %finish.3 = bf16[3,32,128,384]{3,2,1,0:T(8,128)(2,1)} custom-call(f32[2,32]{1,0:T(2,128)} %profile_ref.3, bf16[384,384]{1,0:T(8,128)(2,1)} %maximum_maximum_fusion.stream_ref, bf16[16,392,384]{2,1,0:T(8,128)(2,1)} %all-to-all-done.1.home_ref, bf16[3,32,128,384]{3,2,1,0:T(8,128)(2,1)} %get-tuple-element.11.refs_0_.near_ref, ...), custom_call_target="tpu_custom_call", output_to_operand_aliasing={{}: (5, {})} | custom-call | bytes 17301504 | tf_op jit(solution)/shard_map/finish/pallas_call | solution.py:260
  (30 shorter events, 5.5 us)
Async XLA Ops:
  13.9 211.4 %all-to-all-start.2 = ((bf16[16,4,6,32,384]{4,3,2,1,0:T(8,128)(2,1)}), bf16[16,4,6,32,384]{4,3,2,1,0:T(8,128)(2,1)}, u32[]{:S(2)}, u32[]{:S(2)}) async-start(bf16[16,4,6,32,384]{4,3,2,1,0:T(8,128)(2,1)} %bitcast.14), calls=%async_computation.2 | async-start | bytes 18874368 | tf_op jit(solution)/shard_map/all_to_all | solution.py:340
  29.8 103.3 %collective-permute-start = (bf16[3,16,128,384]{3,2,1,0:T(8,128)(2,1)}, bf16[3,16,128,384]{3,2,1,0:T(8,128)(2,1)S(1)}, u32[]{:S(2)}, u32[]{:S(2)}) collective-permute-start(bf16[3,16,128,384]{3,2,1,0:T(8,128)(2,1)} %get-tuple-element.14), channel_id=1, source_target_pairs={{1,0},{0,1},{3,2},{2,3},{5,4},{4,5},{7,6},{6,7},{9,8},{8,9},{11,10... | collective-permute-start | bytes 14155784 | tf_op jit(solution)/shard_map/ppermute | solution.py:317
  133.2 2.1 copy-start
  225.3 209.7 %all-to-all-start = ((bf16[16,4,6,32,384]{4,3,2,1,0:T(8,128)(2,1)}), bf16[16,4,6,32,384]{4,3,2,1,0:T(8,128)(2,1)}, u32[]{:S(2)}, u32[]{:S(2)}) async-start(bf16[16,4,6,32,384]{4,3,2,1,0:T(8,128)(2,1)} %bitcast.15), calls=%async_computation | async-start | bytes 18874368 | tf_op jit(solution)/shard_map/all_to_all | solution.py:340
  230.2 103.3 %collective-permute-start.1 = (bf16[3,16,128,384]{3,2,1,0:T(8,128)(2,1)}, bf16[3,16,128,384]{3,2,1,0:T(8,128)(2,1)S(1)}, u32[]{:S(2)}, u32[]{:S(2)}) collective-permute-start(bf16[3,16,128,384]{3,2,1,0:T(8,128)(2,1)} %get-tuple-element.13), channel_id=1, source_target_pairs={{1,0},{0,1},{3,2},{2,3},{5,4},{4,5},{7,6},{6,7},{9,8},{8,9},{11,10... | collective-permute-start | bytes 14155784 | tf_op jit(solution)/shard_map/ppermute | solution.py:317
  333.5 2.2 copy-start.2
  350.4 89.6 %copy-start.5 = (bf16[256,256]{1,0:T(8,128)(2,1)S(1)}, bf16[256,256]{1,0:T(8,128)(2,1)}, u32[]{:S(2)}) copy-start(bf16[256,256]{1,0:T(8,128)(2,1)} %param.19) | copy-start | bytes 393220
  350.4 90.5 %copy-start.6 = (bf16[3,128,128]{2,1,0:T(8,128)(2,1)S(1)}, bf16[3,128,128]{2,1,0:T(8,128)(2,1)}, u32[]{:S(2)}) copy-start(bf16[3,128,128]{2,1,0:T(8,128)(2,1)} %param.15) | copy-start | bytes 294916
  350.4 90.6 %copy-start.7 = (bf16[3,128,128]{2,1,0:T(8,128)(2,1)S(1)}, bf16[3,128,128]{2,1,0:T(8,128)(2,1)}, u32[]{:S(2)}) copy-start(bf16[3,128,128]{2,1,0:T(8,128)(2,1)} %param.16) | copy-start | bytes 294916
  350.4 90.7 %copy-start.8 = (bf16[256,256]{1,0:T(8,128)(2,1)S(1)}, bf16[256,256]{1,0:T(8,128)(2,1)}, u32[]{:S(2)}) copy-start(bf16[256,256]{1,0:T(8,128)(2,1)} %param.20) | copy-start | bytes 393220
  435.0 110.7 %all-to-all-start.3 = ((bf16[16,392,384]{2,1,0:T(8,128)(2,1)}), bf16[16,392,384]{2,1,0:T(8,128)(2,1)}, u32[]{:S(2)}, u32[]{:S(2)}) async-start(bf16[16,392,384]{2,1,0:T(8,128)(2,1)} %normal.3), calls=%async_computation.3 | async-start | bytes 9633792 | tf_op jit(solution)/shard_map/all_to_all | solution.py:378
  441.1 1.2 copy-start.4
  500.4 50.3 %copy-start.3 = (bf16[32,128,384]{2,1,0:T(8,128)(2,1)S(1)}, bf16[32,128,384]{2,1,0:T(8,128)(2,1)}, u32[]{:S(2)}) copy-start(bf16[32,128,384]{2,1,0:T(8,128)(2,1)} %get-tuple-element.12) | copy-start | bytes 9437188
  545.8 110.7 %all-to-all-start.1 = ((bf16[16,392,384]{2,1,0:T(8,128)(2,1)}), bf16[16,392,384]{2,1,0:T(8,128)(2,1)}, u32[]{:S(2)}, u32[]{:S(2)}) async-start(bf16[16,392,384]{2,1,0:T(8,128)(2,1)} %normal.2), calls=%async_computation.1 | async-start | bytes 9633792 | tf_op jit(solution)/shard_map/all_to_all | solution.py:378
  550.7 69.5 %collective-permute-start.2 = (bf16[32,128,384]{2,1,0:T(8,128)(2,1)S(1)}, bf16[32,128,384]{2,1,0:T(8,128)(2,1)S(1)}, u32[]{:S(2)}, u32[]{:S(2)}) collective-permute-start(bf16[32,128,384]{2,1,0:T(8,128)(2,1)S(1)} %copy-done.3), channel_id=1, source_target_pairs={{0,1},{1,0},{2,3},{3,2},{4,5},{5,4},{6,7},{7,6},{8,9},{9,8},{10,11... | collective-permute-start | bytes 9437192 | tf_op jit(solution)/shard_map/ppermute | solution.py:370
  620.2 1.6 copy-start.1

commit v2 on v1

--- a/solution.py
+++ b/solution.py
@@ -34,8 +34,8 @@
 
 
 def prepare_kernel(weight_ref, base_ref, step_ref, adjoint_ref, *refs):
-    sent_ref, turned = refs[-2:]
-    rows, planes, cells = base_ref.shape[1:]
+    sent_ref = refs[-1]
+    cells = base_ref.shape[3]
     weight = weight_ref[0]
     for part in range(cells // LANES):
         lanes = pl.ds(part * LANES, LANES)
@@ -43,14 +43,9 @@
             component = field % 3
             if field < 3:
                 value = mixed(weight, base_ref[component, :, :, lanes], step_ref[component, :, :, lanes])
-                value = value.astype(F32)
             else:
-                value = adjoint_ref[component, :, :, lanes].astype(F32)
-            turned[field % 2] = value.reshape(rows * planes, LANES)
-            for plane in range(planes):
-                sent_ref[plane, field, :, lanes] = turned[
-                    field % 2, pl.ds(plane, rows, stride=planes), :
-                ].astype(BF16)
+                value = adjoint_ref[component, :, :, lanes]
+            sent_ref[:, field, :, lanes] = jnp.swapaxes(value, 0, 1)
 
 
 def prepare(weight, base, step, adjoint, earlier, first, count, width):
@@ -64,7 +59,6 @@
         in_specs=[scalars, source, source, source] + [unread()] * len(earlier),
         out_specs=pl.BlockSpec((width, 6, rows, cells), lambda i: (i, 0, 0, 0)),
         out_shape=jax.ShapeDtypeStruct((count, 6, rows, cells), BF16),
-        scratch_shapes=[pltpu.VMEM((2, rows * width, LANES), F32)],
         compiler_params=params(),
         cost_estimate=cost(0, 30 * count * rows * cells),
         name="prepare",
@@ -204,6 +198,10 @@
     )(*operands)
 
 
+def pitched(size):
+    return size + 8 * (1 - size // 8 % 2)
+
+
 def finish_kernel(partials, planes, profile_ref, stream_ref, home_ref, near_ref, *refs):
     partial_refs = refs[:partials]
     out_ref, turned, strips, slopes = refs[-4:]
@@ -224,11 +222,12 @@
             slot = component % 2
             for plane in range(width):
                 place = (3 * (plane % planes) + component) * rows
-                turned[slot, plane * rows : (plane + 1) * rows, :] = home_ref[
+                turned[slot, plane, :rows, :] = home_ref[
                     plane // planes, place : place + rows, lanes
                 ].astype(F32)
+            flat = turned.at[slot].reshape(width * pitched(rows), LANES)
             for row in range(rows):
-                total = turned[slot, pl.ds(row, width, stride=rows), :]
+                total = flat[pl.ds(row, width, stride=pitched(rows)), :]
                 total += near_ref[component, row, :, lanes].astype(F32)
                 if component == 0:
                     total += profile_ref[0, row] * lower + profile_ref[1, row] * upper
@@ -264,7 +263,7 @@
         out_specs=field,
         out_shape=jax.ShapeDtypeStruct(near_term.shape, BF16),
         scratch_shapes=[
-            pltpu.VMEM((2, rows * width, LANES), F32),
+            pltpu.VMEM((2, width, pitched(rows), LANES), F32),
             pltpu.VMEM((held * strip_rows(planes), cells), F32),
             pltpu.VMEM((held * strip_rows(planes), LANES), F32),
         ],
@@ -290,6 +289,10 @@
     if planes < 2:
         return [planes]
     return [planes - planes // 2, planes // 2]
+
+
+def step_width(start, count):
+    return next(width for width in (32, 16, 8) if start % width == 0 and count % width == 0)
 
 
 def per_device(
@@ -308,7 +311,6 @@
     _, rows, planes, cells = base_velocity.shape
     owners = normal_first.shape[0] // rows
     parts = spanwise_first.shape[0] // planes
-    width = 16
     slab = lax.axis_index("col")
 
     def from_others(start, count):
@@ -333,7 +335,7 @@
             others[0] if sent else [],
             start,
             owners * chunk,
-            width,
+            16,
         )
         sent.append(block.reshape(owners, chunk, 6, rows, cells))
 
@@ -379,7 +381,7 @@
     result = None
     for block, start, chunk in zip(returned, starts, chunks):
         result = finish(
-            wall_profile, stream_first, block, near_term, partials, result, start, chunk, width
+            wall_profile, stream_first, block, near_term, partials, result, start, chunk, step_width(start, owners * chunk)
         )
     return result
 

time: 668 us -> 662 us (level)
  Pallas kernels: 120 us -> 108 us
where the time goes in v2:
time: 662 us; the launch traced here: 661 us
  waiting for transfers between devices  509 us (77%)
  Pallas kernels  108 us (16%)
  starting transfers between devices  25.1 us (4%)
  local copies, waits for them, and re-layouts  15.3 us (2%)
    ppermute x2, waiting for transfers between devices, from_others(): lax.ppermute(piece, 'col', [((i + shift) % parts, i) for i in range(parts)])  204 us
    all_to_all x2, waiting for transfers between devices, per_device(): lax.all_to_all(block, 'row', 0, 0, tiled=True)  164 us
    all_to_all x2, waiting for transfers between devices, per_device(): returned.append(lax.all_to_all(term, 'row', 0, 0, tiled=True))  72.9 us
    ppermute x1, waiting for transfers between devices, per_device(): lax.ppermute(partial, 'col', [(i, (i + shift) % parts) for i in range(par...  67.4 us
    pallas_call x2, Pallas kernels, near(): pl.pallas_call(functools.partial(near_kernel, parts), grid=(count,), in_s...  43.4 us
    pallas_call x2, Pallas kernels, normal(): pl.pallas_call(functools.partial(normal_kernel, planes), grid=(planes,),...  29.4 us
    pallas_call x2, Pallas kernels, prepare(): pl.pallas_call(prepare_kernel, grid=(count // width,), in_specs=[scalars,...  20.7 us
    pallas_call x2, Pallas kernels, finish(): pl.pallas_call(functools.partial(finish_kernel, len(partials), planes), g...  14.4 us
  transfers between devices with their start and end apart: 7, of which 7 were waited for; matrix products, arithmetic and copies ran while one was open for 2% of the time, Pallas kernels for 14%

profile of v2, /device:TPU:11, one launch (start us, length us, event | category | flops | bytes accessed | tf_op | source)
XLA Modules:
  0.0 660.8 jit_solution(5082711565542299762)
XLA Ops:
  0.7 10.4 %prepare.3 = bf16[64,6,32,384]{3,2,1,0:T(8,128)(2,1)} custom-call(f32[1]{0:T(128)S(6)} %copy.23.weight_ref, bf16[3,32,128,384]{3,2,1,0:T(8,128)(2,1)} %base_ref.7, bf16[3,32,128,384]{3,2,1,0:T(8,128)(2,1)} %step_ref.7, bf16[3,32,128,384]{3,2,1,0:T(8,128)(2,1)} %adjoint_ref.3), custom_call_target="tpu_custom_call" | custom-call | bytes 23592960 | tf_op jit(solution)/shard_map/prepare/pallas_call | solution.py:56
  11.1 6.6 all-to-all-start.2
  17.6 9.3 %fusion.4 = (bf16[3,16,128,384]{3,2,1,0:T(8,128)(2,1)}, bf16[3,16,128,384]{3,2,1,0:T(8,128)(2,1)}) fusion(bf16[3,32,128,384]{3,2,1,0:T(8,128)(2,1)} %adjoint_ref.3), kind=kLoop, calls=%fused_computation.26 | loop fusion | bytes 18874368 | tf_op jit(solution)/shard_map/slice | solution.py:317
  28.2 102.1 %collective-permute-done.refs_0_.refs_1_ = bf16[3,16,128,384]{3,2,1,0:T(8,128)(2,1)S(1)} collective-permute-done((bf16[3,16,128,384]{3,2,1,0:T(8,128)(2,1)}, bf16[3,16,128,384]{3,2,1,0:T(8,128)(2,1)S(1)}, u32[]{:S(2)}, u32[]{:S(2)}) %collective-permute-start) | collective-permute-done | bytes 4718624 | tf_op jit(solution)/shard_map/ppermute | solution.py:319
  130.3 2.1 copy-done
  132.4 10.3 %prepare.2 = bf16[64,6,32,384]{3,2,1,0:T(8,128)(2,1)} custom-call(f32[1]{0:T(128)S(6)} %copy.23.weight_ref, bf16[3,32,128,384]{3,2,1,0:T(8,128)(2,1)} %base_ref.7, bf16[3,32,128,384]{3,2,1,0:T(8,128)(2,1)} %step_ref.7, bf16[3,32,128,384]{3,2,1,0:T(8,128)(2,1)} %adjoint_ref.3, bf16[3,16,128,384]{3,2,1,0:T(8,128)(2,1)} %copy-done), custom_call_target="tpu_custom_call" | custom-call | bytes 23592960 | tf_op jit(solution)/shard_map/prepare/pallas_call | solution.py:56
  142.7 79.7 %all-to-all-done.2.lines_ref = bf16[16,4,6,32,384]{4,3,2,1,0:T(8,128)(2,1)} async-done(((bf16[16,4,6,32,384]{4,3,2,1,0:T(8,128)(2,1)}), bf16[16,4,6,32,384]{4,3,2,1,0:T(8,128)(2,1)}, u32[]{:S(2)}, u32[]{:S(2)}) %all-to-all-start.2) | async-done | bytes 9437216 | tf_op jit(solution)/shard_map/all_to_all | solution.py:342
  222.4 4.9 all-to-all-start
  228.6 102.0 %collective-permute-done.1.refs_1_.refs_0_ = bf16[3,16,128,384]{3,2,1,0:T(8,128)(2,1)S(1)} collective-permute-done((bf16[3,16,128,384]{3,2,1,0:T(8,128)(2,1)}, bf16[3,16,128,384]{3,2,1,0:T(8,128)(2,1)S(1)}, u32[]{:S(2)}, u32[]{:S(2)}) %collective-permute-start.1) | collective-permute-done | bytes 4718624 | tf_op jit(solution)/shard_map/ppermute | solution.py:319
  330.6 2.2 copy-done.2
  332.8 14.7 %normal.3 = bf16[16,392,384]{2,1,0:T(8,128)(2,1)} custom-call(bf16[512,512]{1,0:T(8,128)(2,1)} %first_ref.3, bf16[512,512]{1,0:T(8,128)(2,1)} %second_ref.3, bf16[16,4,6,32,384]{4,3,2,1,0:T(8,128)(2,1)} %all-to-all-done.2.lines_ref, bf16[3,16,128,384]{3,2,1,0:T(8,128)(2,1)} %copy-done.2), custom_call_target="tpu_custom_call" | custom-call | flops 7247757312 | bytes 14155776 | tf_op jit(solution)/shard_map/normal/pallas_call | solution.py:117
  347.5 84.6 %all-to-all-done.lines_ref = bf16[16,4,6,32,384]{4,3,2,1,0:T(8,128)(2,1)} async-done(((bf16[16,4,6,32,384]{4,3,2,1,0:T(8,128)(2,1)}), bf16[16,4,6,32,384]{4,3,2,1,0:T(8,128)(2,1)}, u32[]{:S(2)}, u32[]{:S(2)}) %all-to-all-start) | async-done | bytes 9437216 | tf_op jit(solution)/shard_map/all_to_all | solution.py:342
  432.2 4.9 all-to-all-start.3
  439.4 21.7 %near.2 = (bf16[3,32,128,384]{3,2,1,0:T(8,128)(2,1)}, bf16[32,128,384]{2,1,0:T(8,128)(2,1)}) custom-call(f32[1]{0:T(128)S(6)} %copy.23.weight_ref, bf16[384,768]{1,0:T(8,128)(2,1)} %copy-done.4, bf16[256,256]{1,0:T(8,128)(2,1)} %fusion.1.curve_ref, bf16[256,128]{1,0:T(8,128)(2,1)} %fusion.3.cross_ref, bf16[3,32,128,384]{3,2,1,0:T(8,128)(2,1)} %base_ref.7, ...), custom_call_target="tpu_custom_call" | custom-call | flops 9059696640 | bytes 28311552 | tf_op jit(solution)/shard_map/near/pallas_call | solution.py:181
  461.1 21.7 %near.3 = (bf16[3,32,128,384]{3,2,1,0:T(8,128)(2,1)}, bf16[32,128,384]{2,1,0:T(8,128)(2,1)}) custom-call(f32[1]{0:T(128)S(6)} %copy.23.weight_ref, bf16[384,768]{1,0:T(8,128)(2,1)} %copy-done.4, bf16[256,256]{1,0:T(8,128)(2,1)} %fusion.1.curve_ref, bf16[256,128]{1,0:T(8,128)(2,1)} %fusion.3.cross_ref, ...), custom_call_target="tpu_custom_call", output_to_operand_aliasing={{0}: (8, {}), {1}: (9, {})} | custom-call | flops 9059696640 | bytes 28311552 | tf_op jit(solution)/shard_map/near/pallas_call | solution.py:181
  482.9 14.6 %normal.2 = bf16[16,392,384]{2,1,0:T(8,128)(2,1)} custom-call(bf16[512,512]{1,0:T(8,128)(2,1)} %first_ref.3, bf16[512,512]{1,0:T(8,128)(2,1)} %second_ref.3, bf16[16,4,6,32,384]{4,3,2,1,0:T(8,128)(2,1)} %all-to-all-done.lines_ref, bf16[3,32,128,384]{3,2,1,0:T(8,128)(2,1)} %get-tuple-element.11.refs_0_.near_ref), custom_call_target="tpu_custom_call" | custom-call | flops 7247757312 | bytes 14155776 | tf_op jit(solution)/shard_map/normal/pallas_call | solution.py:117
  497.5 45.4 %all-to-all-done.3.home_ref = bf16[16,392,384]{2,1,0:T(8,128)(2,1)} async-done(((bf16[16,392,384]{2,1,0:T(8,128)(2,1)}), bf16[16,392,384]{2,1,0:T(8,128)(2,1)}, u32[]{:S(2)}, u32[]{:S(2)}) %all-to-all-start.3) | async-done | bytes 4816928 | tf_op jit(solution)/shard_map/all_to_all | solution.py:380
  542.9 4.9 all-to-all-start.1
  547.8 1.3 collective-permute-start.2
  549.9 67.4 %collective-permute-done.2.refs_0_ = bf16[32,128,384]{2,1,0:T(8,128)(2,1)S(1)} collective-permute-done((bf16[32,128,384]{2,1,0:T(8,128)(2,1)S(1)}, bf16[32,128,384]{2,1,0:T(8,128)(2,1)S(1)}, u32[]{:S(2)}, u32[]{:S(2)}) %collective-permute-start.2) | collective-permute-done | bytes 3145760 | tf_op jit(solution)/shard_map/ppermute | solution.py:372
  617.3 1.6 copy-done.1
  618.9 7.2 %finish.2.refs_1_ = bf16[3,32,128,384]{3,2,1,0:T(8,128)(2,1)} custom-call(f32[2,32]{1,0:T(2,128)} %profile_ref.3, bf16[384,384]{1,0:T(8,128)(2,1)} %maximum_maximum_fusion.stream_ref, bf16[16,392,384]{2,1,0:T(8,128)(2,1)} %all-to-all-done.3.home_ref, bf16[3,32,128,384]{3,2,1,0:T(8,128)(2,1)} %get-tuple-element.11.refs_0_.near_ref, ...), custom_call_target="tpu_custom_call" | custom-call | bytes 17301504 | tf_op jit(solution)/shard_map/finish/pallas_call | solution.py:259
  626.1 27.5 %all-to-all-done.1.home_ref = bf16[16,392,384]{2,1,0:T(8,128)(2,1)} async-done(((bf16[16,392,384]{2,1,0:T(8,128)(2,1)}), bf16[16,392,384]{2,1,0:T(8,128)(2,1)}, u32[]{:S(2)}, u32[]{:S(2)}) %all-to-all-start.1) | async-done | bytes 4816928 | tf_op jit(solution)/shard_map/all_to_all | solution.py:380
  653.6 7.2 %finish.3 = bf16[3,32,128,384]{3,2,1,0:T(8,128)(2,1)} custom-call(f32[2,32]{1,0:T(2,128)} %profile_ref.3, bf16[384,384]{1,0:T(8,128)(2,1)} %maximum_maximum_fusion.stream_ref, bf16[16,392,384]{2,1,0:T(8,128)(2,1)} %all-to-all-done.1.home_ref, bf16[3,32,128,384]{3,2,1,0:T(8,128)(2,1)} %get-tuple-element.11.refs_0_.near_ref, ...), custom_call_target="tpu_custom_call", output_to_operand_aliasing={{}: (5, {})} | custom-call | bytes 17301504 | tf_op jit(solution)/shard_map/finish/pallas_call | solution.py:259
  (30 shorter events, 5.5 us)
Async XLA Ops:
  11.1 211.4 %all-to-all-start.2 = ((bf16[16,4,6,32,384]{4,3,2,1,0:T(8,128)(2,1)}), bf16[16,4,6,32,384]{4,3,2,1,0:T(8,128)(2,1)}, u32[]{:S(2)}, u32[]{:S(2)}) async-start(bf16[16,4,6,32,384]{4,3,2,1,0:T(8,128)(2,1)} %bitcast.14), calls=%async_computation.2 | async-start | bytes 18874368 | tf_op jit(solution)/shard_map/all_to_all | solution.py:342
  27.0 103.3 %collective-permute-start = (bf16[3,16,128,384]{3,2,1,0:T(8,128)(2,1)}, bf16[3,16,128,384]{3,2,1,0:T(8,128)(2,1)S(1)}, u32[]{:S(2)}, u32[]{:S(2)}) collective-permute-start(bf16[3,16,128,384]{3,2,1,0:T(8,128)(2,1)} %get-tuple-element.14), channel_id=1, source_target_pairs={{1,0},{0,1},{3,2},{2,3},{5,4},{4,5},{7,6},{6,7},{9,8},{8,9},{11,10... | collective-permute-start | bytes 14155784 | tf_op jit(solution)/shard_map/ppermute | solution.py:319
  130.3 2.1 copy-start
  222.4 209.7 %all-to-all-start = ((bf16[16,4,6,32,384]{4,3,2,1,0:T(8,128)(2,1)}), bf16[16,4,6,32,384]{4,3,2,1,0:T(8,128)(2,1)}, u32[]{:S(2)}, u32[]{:S(2)}) async-start(bf16[16,4,6,32,384]{4,3,2,1,0:T(8,128)(2,1)} %bitcast.15), calls=%async_computation | async-start | bytes 18874368 | tf_op jit(solution)/shard_map/all_to_all | solution.py:342
  227.4 103.3 %collective-permute-start.1 = (bf16[3,16,128,384]{3,2,1,0:T(8,128)(2,1)}, bf16[3,16,128,384]{3,2,1,0:T(8,128)(2,1)S(1)}, u32[]{:S(2)}, u32[]{:S(2)}) collective-permute-start(bf16[3,16,128,384]{3,2,1,0:T(8,128)(2,1)} %get-tuple-element.13), channel_id=1, source_target_pairs={{1,0},{0,1},{3,2},{2,3},{5,4},{4,5},{7,6},{6,7},{9,8},{8,9},{11,10... | collective-permute-start | bytes 14155784 | tf_op jit(solution)/shard_map/ppermute | solution.py:319
  330.6 2.2 copy-start.2
  347.5 89.6 %copy-start.5 = (bf16[256,256]{1,0:T(8,128)(2,1)S(1)}, bf16[256,256]{1,0:T(8,128)(2,1)}, u32[]{:S(2)}) copy-start(bf16[256,256]{1,0:T(8,128)(2,1)} %param.19) | copy-start | bytes 393220
  347.5 90.5 %copy-start.6 = (bf16[3,128,128]{2,1,0:T(8,128)(2,1)S(1)}, bf16[3,128,128]{2,1,0:T(8,128)(2,1)}, u32[]{:S(2)}) copy-start(bf16[3,128,128]{2,1,0:T(8,128)(2,1)} %param.15) | copy-start | bytes 294916
  347.5 90.6 %copy-start.7 = (bf16[3,128,128]{2,1,0:T(8,128)(2,1)S(1)}, bf16[3,128,128]{2,1,0:T(8,128)(2,1)}, u32[]{:S(2)}) copy-start(bf16[3,128,128]{2,1,0:T(8,128)(2,1)} %param.16) | copy-start | bytes 294916
  347.5 90.7 %copy-start.8 = (bf16[256,256]{1,0:T(8,128)(2,1)S(1)}, bf16[256,256]{1,0:T(8,128)(2,1)}, u32[]{:S(2)}) copy-start(bf16[256,256]{1,0:T(8,128)(2,1)} %param.20) | copy-start | bytes 393220
  432.2 110.7 %all-to-all-start.3 = ((bf16[16,392,384]{2,1,0:T(8,128)(2,1)}), bf16[16,392,384]{2,1,0:T(8,128)(2,1)}, u32[]{:S(2)}, u32[]{:S(2)}) async-start(bf16[16,392,384]{2,1,0:T(8,128)(2,1)} %normal.3), calls=%async_computation.3 | async-start | bytes 9633792 | tf_op jit(solution)/shard_map/all_to_all | solution.py:380
  438.2 1.2 copy-start.4
  497.5 50.3 %copy-start.3 = (bf16[32,128,384]{2,1,0:T(8,128)(2,1)S(1)}, bf16[32,128,384]{2,1,0:T(8,128)(2,1)}, u32[]{:S(2)}) copy-start(bf16[32,128,384]{2,1,0:T(8,128)(2,1)} %get-tuple-element.12) | copy-start | bytes 9437188
  542.9 110.7 %all-to-all-start.1 = ((bf16[16,392,384]{2,1,0:T(8,128)(2,1)}), bf16[16,392,384]{2,1,0:T(8,128)(2,1)}, u32[]{:S(2)}, u32[]{:S(2)}) async-start(bf16[16,392,384]{2,1,0:T(8,128)(2,1)} %normal.2), calls=%async_computation.1 | async-start | bytes 9633792 | tf_op jit(solution)/shard_map/all_to_all | solution.py:380
  547.8 69.5 %collective-permute-start.2 = (bf16[32,128,384]{2,1,0:T(8,128)(2,1)S(1)}, bf16[32,128,384]{2,1,0:T(8,128)(2,1)S(1)}, u32[]{:S(2)}, u32[]{:S(2)}) collective-permute-start(bf16[32,128,384]{2,1,0:T(8,128)(2,1)S(1)} %copy-done.3), channel_id=1, source_target_pairs={{0,1},{1,0},{2,3},{3,2},{4,5},{5,4},{6,7},{7,6},{8,9},{9,8},{10,11... | collective-permute-start | bytes 9437192 | tf_op jit(solution)/shard_map/ppermute | solution.py:372
  617.3 1.6 copy-start.1

commit v3 on v2

--- a/solution.py
+++ b/solution.py
@@ -33,9 +33,9 @@
     return (base.astype(F32) + weight * step.astype(F32)).astype(BF16)
 
 
-def prepare_kernel(weight_ref, base_ref, step_ref, adjoint_ref, *refs):
+def prepare_kernel(planes, profiles, weight_ref, base_ref, step_ref, adjoint_ref, *refs):
     sent_ref = refs[-1]
-    cells = base_ref.shape[3]
+    rows, width, cells = base_ref.shape[1:]
     weight = weight_ref[0]
     for part in range(cells // LANES):
         lanes = pl.ds(part * LANES, LANES)
@@ -45,42 +45,49 @@
                 value = mixed(weight, base_ref[component, :, :, lanes], step_ref[component, :, :, lanes])
             else:
                 value = adjoint_ref[component, :, :, lanes]
-            sent_ref[:, field, :, lanes] = jnp.swapaxes(value, 0, 1)
-
-
-def prepare(weight, base, step, adjoint, earlier, first, count, width):
+            value = jnp.swapaxes(value, 0, 1)
+            for plane in range(width):
+                place = (6 * (plane % planes) + field) * rows
+                sent_ref[plane // planes, place : place + rows, lanes] = value[plane]
+    if profiles:
+        rest = refs[0][...]
+        pieces = []
+        for _ in range(3):
+            pieces.append(rest.astype(BF16).astype(F32))
+            rest = rest - pieces[-1]
+        pieces.append(jnp.zeros_like(rest))
+        joined = jnp.concatenate(pieces, axis=0).astype(BF16)
+        for owner in range(width // planes):
+            sent_ref[owner, 6 * planes * rows :, :rows] = joined
+
+
+def prepare(weight, base, step, adjoint, profiles, earlier, first, owners, planes, width):
     _, rows, _, cells = base.shape
     start = first // width
     source = pl.BlockSpec((3, rows, width, cells), lambda i: (0, 0, start + i, 0))
-    scalars = pl.BlockSpec(memory_space=pltpu.SMEM)
+    length = 6 * planes * rows + 8 * len(profiles)
     return pl.pallas_call(
-        prepare_kernel,
-        grid=(count // width,),
-        in_specs=[scalars, source, source, source] + [unread()] * len(earlier),
-        out_specs=pl.BlockSpec((width, 6, rows, cells), lambda i: (i, 0, 0, 0)),
-        out_shape=jax.ShapeDtypeStruct((count, 6, rows, cells), BF16),
+        functools.partial(prepare_kernel, planes, len(profiles)),
+        grid=(owners * planes // width,),
+        in_specs=[pl.BlockSpec(memory_space=pltpu.SMEM), source, source, source]
+        + [resident(profile.shape) for profile in profiles]
+        + [unread()] * len(earlier),
+        out_specs=pl.BlockSpec((width // planes, length, cells), lambda i: (i, 0, 0)),
+        out_shape=jax.ShapeDtypeStruct((owners, length, cells), BF16),
         compiler_params=params(),
-        cost_estimate=cost(0, 30 * count * rows * cells),
+        cost_estimate=cost(0, 30 * owners * planes * rows * cells),
         name="prepare",
-    )(weight, base, step, adjoint, *earlier)
-
-
-def strip_rows(planes):
-    return next(total for total in range(8, 16 * planes + 8, 8) if total % planes == 0 and total >= 2 * planes)
-
-
-def normal_kernel(planes, first_ref, second_ref, lines_ref, *refs):
+    )(weight, base, step, adjoint, *profiles, *earlier)
+
+
+def normal_kernel(first_ref, second_ref, stream_ref, profile_ref, lines_ref, *refs):
     out_ref, strips = refs[-2:]
-    owners, _, _, rows, cells = lines_ref.shape
+    owners, length, cells = lines_ref.shape
+    rows = length // 6
     lines = owners * rows
-    plane = pl.program_id(0)
 
     def whole(field):
-        return lines_ref[:, 0, field].reshape(lines, cells)
-
-    @pl.when(plane == 0)
-    def _():
-        strips[...] = jnp.zeros_like(strips)
+        return lines_ref[:, field * rows : (field + 1) * rows, :].reshape(lines, cells)
 
     first = first_ref[...]
     second = second_ref[...]
@@ -88,48 +95,42 @@
     for component in range(3):
         slope = jnp.dot(first, whole(component), preferred_element_type=F32)
         if component == 0:
-            place = plane * (strips.shape[0] // planes)
-            strips[pl.ds(place, 1), :] = slope[:1]
-            strips[pl.ds(place + 1, 1), :] = slope[lines - 1 :]
+            strips[...] = jnp.zeros_like(strips)
+            strips[:1, :] = slope[:1]
+            strips[1:2, :] = slope[lines - 1 :]
         term = whole(3 + component).astype(F32) * slope
         cross = term if cross is None else cross + term
+    wall_shear = strips[...].astype(BF16)
+    shear_slope = jnp.dot(wall_shear, stream_ref[...], preferred_element_type=F32)
     speed = whole(1).astype(F32)
     for component in range(3):
         field = whole(3 + component)
         slope = jnp.dot(first, field, preferred_element_type=F32)
         term = jnp.dot(second, field, preferred_element_type=F32) - speed * slope
+        if component == 0:
+            term += profile_ref[:, :1] * shear_slope[:1] + profile_ref[:, 1:] * shear_slope[1:2]
         if component == 1:
-            term = term + cross
-        place = pl.multiple_of((3 * plane + component) * rows, rows)
-        out_ref[:, pl.ds(place, rows), :] = term.astype(BF16).reshape(owners, rows, cells)
-
-    @pl.when(plane == planes - 1)
-    def _():
-        last = strips[...].astype(BF16)
-        for owner in range(owners):
-            out_ref[owner, 3 * planes * rows :, :] = last
-
-
-def normal(first_op, second_op, received, earlier):
-    owners, planes, _, rows, cells = received.shape
-    lines = owners * rows
-    length = 3 * planes * rows + strip_rows(planes)
+            term += cross
+        out_ref[:, 0, component] = term.astype(BF16).reshape(owners, rows, cells)
+
+
+def normal(first_op, second_op, stream, profile, received, planes, earlier):
+    owners, _, cells = received.shape
+    lines = first_op.shape[0]
+    rows = lines // owners
     return pl.pallas_call(
-        functools.partial(normal_kernel, planes),
+        normal_kernel,
         grid=(planes,),
-        in_specs=[
-            resident((lines, lines)),
-            resident((lines, lines)),
-            pl.BlockSpec((owners, 1, 6, rows, cells), lambda p: (0, p, 0, 0, 0)),
-        ]
+        in_specs=[resident(operand.shape) for operand in (first_op, second_op, stream, profile)]
+        + [pl.BlockSpec((owners, 6 * rows, cells), lambda p: (0, p, 0))]
         + [unread()] * len(earlier),
-        out_specs=resident((owners, length, cells)),
-        out_shape=jax.ShapeDtypeStruct((owners, length, cells), BF16),
-        scratch_shapes=[pltpu.VMEM((strip_rows(planes), cells), F32)],
+        out_specs=pl.BlockSpec((owners, 1, 3, rows, cells), lambda p: (0, p, 0, 0, 0)),
+        out_shape=jax.ShapeDtypeStruct((owners, planes, 3, rows, cells), BF16),
+        scratch_shapes=[pltpu.VMEM((16, cells), F32)],
         compiler_params=params(),
         cost_estimate=cost(18 * planes * lines * lines * cells, 18 * planes * lines * cells),
         name="normal",
-    )(first_op, second_op, received, *earlier)
+    )(first_op, second_op, stream, profile, received, *earlier)
 
 
 def near_kernel(parts, weight_ref, stream_ref, curve_ref, cross_ref, base_ref, step_ref, *refs):
@@ -166,10 +167,9 @@
         near_ref[c, 0] = total.astype(BF16)
 
 
-def near(weight, stream, curve, cross, base, step, own, others, previous, first):
+def near(weight, stream, curve, cross, base, step, own, others, previous, first, count):
     _, rows, planes, cells = base.shape
     parts = 1 + len(others)
-    count = rows if not others else others[0].shape[1]
     row_of = pl.BlockSpec((3, 1, planes, cells), lambda i: (0, first + i, 0, 0))
     row_one = pl.BlockSpec((1, planes, cells), lambda i: (first + i, 0, 0))
     scalars = pl.BlockSpec(memory_space=pltpu.SMEM)
@@ -202,74 +202,50 @@
     return size + 8 * (1 - size // 8 % 2)
 
 
-def finish_kernel(partials, planes, profile_ref, stream_ref, home_ref, near_ref, *refs):
+def finish_kernel(partials, home_ref, near_ref, *refs):
     partial_refs = refs[:partials]
-    out_ref, turned, strips, slopes = refs[-4:]
-    owners, length, cells = home_ref.shape
-    rows = out_ref.shape[1]
-    width = owners * planes
-    held = length - 3 * planes * rows
-    pitch = held // planes
-    for owner in range(owners):
-        strips[owner * held : (owner + 1) * held, :] = home_ref[owner, 3 * planes * rows :, :].astype(F32)
-    slope = jnp.dot(strips[...].astype(BF16), stream_ref[...], preferred_element_type=F32)
+    out_ref, turned = refs[-2:]
+    width, _, rows, cells = home_ref.shape
+    pitch = pitched(rows)
     for part in range(cells // LANES):
         lanes = pl.ds(part * LANES, LANES)
-        slopes[...] = slope[:, part * LANES : (part + 1) * LANES]
-        lower = slopes[pl.ds(0, width, stride=pitch), :]
-        upper = slopes[pl.ds(1, width, stride=pitch), :]
         for component in range(3):
             slot = component % 2
             for plane in range(width):
-                place = (3 * (plane % planes) + component) * rows
-                turned[slot, plane, :rows, :] = home_ref[
-                    plane // planes, place : place + rows, lanes
-                ].astype(F32)
-            flat = turned.at[slot].reshape(width * pitched(rows), LANES)
+                turned[slot, plane * pitch : plane * pitch + rows, :] = home_ref[plane, component, :, lanes].astype(
+                    F32
+                )
             for row in range(rows):
-                total = flat[pl.ds(row, width, stride=pitched(rows)), :]
+                total = turned[slot, pl.ds(row, width, stride=pitch), :]
                 total += near_ref[component, row, :, lanes].astype(F32)
-                if component == 0:
-                    total += profile_ref[0, row] * lower + profile_ref[1, row] * upper
                 if component == 2:
                     for ref in partial_refs:
                         total += ref[row, :, lanes].astype(F32)
                 out_ref[component, row, :, lanes] = total.astype(BF16)
 
 
-def finish(profile, stream, home, near_term, partials, previous, first, planes, width):
-    owners, length, cells = home.shape
-    rows = near_term.shape[1]
+def finish(home, near_term, partials, previous, first, width):
+    count, _, rows, cells = home.shape
     start = first // width
-    held = width // planes
     field = pl.BlockSpec((3, rows, width, cells), lambda i: (0, 0, start + i, 0))
     single = pl.BlockSpec((rows, width, cells), lambda i: (0, start + i, 0))
-    operands = [profile, stream, home, near_term, *partials]
-    specs = [
-        pl.BlockSpec(memory_space=pltpu.SMEM),
-        resident(stream.shape),
-        pl.BlockSpec((held, length, cells), lambda i: (i, 0, 0)),
-        field,
-    ] + [single] * len(partials)
+    operands = [home, near_term, *partials]
+    specs = [pl.BlockSpec((width, 3, rows, cells), lambda i: (i, 0, 0, 0)), field] + [single] * len(partials)
     aliases = {}
     if previous is not None:
         aliases = {len(operands): 0}
         operands.append(previous)
         specs.append(unread())
     return pl.pallas_call(
-        functools.partial(finish_kernel, len(partials), planes),
-        grid=(owners * planes // width,),
+        functools.partial(finish_kernel, len(partials)),
+        grid=(count // width,),
         in_specs=specs,
         out_specs=field,
         out_shape=jax.ShapeDtypeStruct(near_term.shape, BF16),
-        scratch_shapes=[
-            pltpu.VMEM((2, width, pitched(rows), LANES), F32),
-            pltpu.VMEM((held * strip_rows(planes), cells), F32),
-            pltpu.VMEM((held * strip_rows(planes), LANES), F32),
-        ],
+        scratch_shapes=[pltpu.VMEM((2, width * pitched(rows), LANES), F32)],
         input_output_aliases=aliases,
         compiler_params=params(),
-        cost_estimate=cost(0, 22 * owners * planes * rows * cells),
+        cost_estimate=cost(0, 22 * count * rows * cells),
         name="finish",
     )(*operands)
 
@@ -326,21 +302,26 @@
     chunks = divide(planes // owners)
     starts = [owners * sum(chunks[:k]) for k in range(len(chunks))]
     sent = []
-    for chunk, start in zip(chunks, starts):
-        block = prepare(
-            increment_weight,
-            base_velocity,
-            velocity_step,
-            adjoint_velocity,
-            others[0] if sent else [],
-            start,
-            owners * chunk,
-            16,
+    for number, (chunk, start) in enumerate(zip(chunks, starts)):
+        sent.append(
+            prepare(
+                increment_weight,
+                base_velocity,
+                velocity_step,
+                adjoint_velocity,
+                [wall_profile] if number == 0 else [],
+                others[0] if number == 1 else [],
+                start,
+                owners,
+                chunk,
+                16,
+            )
         )
-        sent.append(block.reshape(owners, chunk, 6, rows, cells))
 
     received = [lax.all_to_all(block, "row", 0, 0, tiled=True) for block in sent]
 
+    pieces = received[0][:, 6 * chunks[0] * rows :, :rows].astype(F32)
+    profile = (pieces[:, 0:2] + pieces[:, 2:4] + pieces[:, 4:6]).transpose(0, 2, 1).reshape(owners * rows, 2)
     stream_first = joined_blocks(streamwise_first, cells)
     stream_second = joined_blocks(streamwise_second, cells)
     stream = jnp.concatenate([stream_first, stream_second], axis=1)
@@ -366,6 +347,7 @@
             pieces,
             local,
             number * half,
+            half,
         )
     near_term, *partials = local
     partials = [
@@ -374,15 +356,15 @@
     ]
 
     returned = []
-    for number, block in enumerate(received):
+    for number, (block, chunk) in enumerate(zip(received, chunks)):
         earlier = others[1] if number == 0 else [near_term]
-        term = normal(normal_first, normal_second, block, earlier)
+        term = normal(normal_first, normal_second, stream_first, profile, block, chunk, earlier)
         returned.append(lax.all_to_all(term, "row", 0, 0, tiled=True))
     result = None
     for block, start, chunk in zip(returned, starts, chunks):
-        result = finish(
-            wall_profile, stream_first, block, near_term, partials, result, start, chunk, step_width(start, owners * chunk)
-        )
+        home = block.reshape(owners * chunk, 3, rows, cells)
+        width = step_width(start, owners * chunk)
+        result = finish(home, near_term, partials, result, start, width)
     return result
 
 

time: 662 us -> 660 us (level)
  no operation moved by 1% of the time
where the time goes in v3:
time: 660 us; the launch traced here: 658 us
  waiting for transfers between devices  509 us (77%)
  Pallas kernels  106 us (16%)
  starting transfers between devices  25.1 us (4%)
  local copies, waits for them, and re-layouts  14.1 us (2%)
    ppermute x2, waiting for transfers between devices, from_others(): lax.ppermute(piece, 'col', [((i + shift) % parts, i) for i in range(parts)])  202 us
    all_to_all x2, waiting for transfers between devices, per_device(): lax.all_to_all(block, 'row', 0, 0, tiled=True)  169 us
    all_to_all x2, waiting for transfers between devices, per_device(): returned.append(lax.all_to_all(term, 'row', 0, 0, tiled=True))  69.4 us
    ppermute x1, waiting for transfers between devices, per_device(): lax.ppermute(partial, 'col', [(i, (i + shift) % parts) for i in range(par...  68.2 us
    pallas_call x2, Pallas kernels, near(): pl.pallas_call(functools.partial(near_kernel, parts), grid=(count,), in_s...  43.4 us
    pallas_call x2, Pallas kernels, normal(): pl.pallas_call(normal_kernel, grid=(planes,), in_specs=[resident(operand....  28.2 us
    pallas_call x2, Pallas kernels, prepare(): pl.pallas_call(functools.partial(prepare_kernel, planes, len(profiles)),...  20.7 us
    pallas_call x2, Pallas kernels, finish(): pl.pallas_call(functools.partial(finish_kernel, len(partials)), grid=(cou...  13.9 us
  transfers between devices with their start and end apart: 7, of which 7 were waited for; matrix products, arithmetic and copies ran while one was open for 2% of the time, Pallas kernels for 14%

profile of v3, /device:TPU:11, one launch (start us, length us, event | category | flops | bytes accessed | tf_op | source)
XLA Modules:
  0.0 658.4 jit_solution(16128816364796716888)
XLA Ops:
  0.7 10.4 %prepare.2 = bf16[16,776,384]{2,1,0:T(8,128)(2,1)} custom-call(f32[1]{0:T(128)S(6)} %copy.28.weight_ref, bf16[3,32,128,384]{3,2,1,0:T(8,128)(2,1)} %base_ref.7, bf16[3,32,128,384]{3,2,1,0:T(8,128)(2,1)} %step_ref.7, bf16[3,32,128,384]{3,2,1,0:T(8,128)(2,1)} %refs_0_.5, f32[2,32]{1,0:T(2,128)} %refs_0_.3), custom_call_target="tpu_custom_call" | custom-call | bytes 23592960 | tf_op jit(solution)/shard_map/prepare/pallas_call | solution.py:69
  11.0 6.6 all-to-all-start
  17.6 9.3 %fusion.5 = (bf16[3,16,128,384]{3,2,1,0:T(8,128)(2,1)}, bf16[3,16,128,384]{3,2,1,0:T(8,128)(2,1)}) fusion(bf16[3,32,128,384]{3,2,1,0:T(8,128)(2,1)} %refs_0_.5), kind=kLoop, calls=%fused_computation.30 | loop fusion | bytes 18874368 | tf_op jit(solution)/shard_map/slice | solution.py:293
  28.2 102.1 %collective-permute-done.refs_0_.refs_1_ = bf16[3,16,128,384]{3,2,1,0:T(8,128)(2,1)S(1)} collective-permute-done((bf16[3,16,128,384]{3,2,1,0:T(8,128)(2,1)}, bf16[3,16,128,384]{3,2,1,0:T(8,128)(2,1)S(1)}, u32[]{:S(2)}, u32[]{:S(2)}) %collective-permute-start) | collective-permute-done | bytes 4718624 | tf_op jit(solution)/shard_map/ppermute | solution.py:295
  130.3 2.1 copy-done
  132.4 10.3 %prepare.3 = bf16[16,768,384]{2,1,0:T(8,128)(2,1)} custom-call(f32[1]{0:T(128)S(6)} %copy.28.weight_ref, bf16[3,32,128,384]{3,2,1,0:T(8,128)(2,1)} %base_ref.7, bf16[3,32,128,384]{3,2,1,0:T(8,128)(2,1)} %step_ref.7, bf16[3,32,128,384]{3,2,1,0:T(8,128)(2,1)} %refs_0_.5, bf16[3,16,128,384]{3,2,1,0:T(8,128)(2,1)} %copy-done), custom_call_target="tpu_custom_call" | custom-call | bytes 23592960 | tf_op jit(solution)/shard_map/prepare/pallas_call | solution.py:69
  142.7 81.8 %all-to-all-done.lines_ref = bf16[16,776,384]{2,1,0:T(8,128)(2,1)} async-done(((bf16[16,776,384]{2,1,0:T(8,128)(2,1)}), bf16[16,776,384]{2,1,0:T(8,128)(2,1)}, u32[]{:S(2)}, u32[]{:S(2)}) %all-to-all-start) | async-done | bytes 9535520 | tf_op jit(solution)/shard_map/all_to_all | solution.py:321
  224.5 4.9 all-to-all-start.1
  229.4 1.2 collective-permute-start.1
  233.1 99.7 %collective-permute-done.1.refs_1_.refs_0_ = bf16[3,16,128,384]{3,2,1,0:T(8,128)(2,1)} collective-permute-done((bf16[3,16,128,384]{3,2,1,0:T(8,128)(2,1)}, bf16[3,16,128,384]{3,2,1,0:T(8,128)(2,1)}, u32[]{:S(2)}, u32[]{:S(2)}) %collective-permute-start.1) | collective-permute-done | bytes 4718624 | tf_op jit(solution)/shard_map/ppermute | solution.py:295
  332.8 14.1 %normal.3 = bf16[16,4,3,32,384]{4,3,2,1,0:T(8,128)(2,1)} custom-call(bf16[512,512]{1,0:T(8,128)(2,1)} %first_ref.3, bf16[512,512]{1,0:T(8,128)(2,1)} %second_ref.3, bf16[384,384]{1,0:T(8,128)(2,1)} %maximum_maximum_fusion.stream_ref, f32[512,2]{1,0:T(8,128)} %bitcast.17, bf16[16,776,384]{2,1,0:T(8,128)(2,1)} %all-to-all-done.lines_ref, ...), custom_call_target="tpu_custom_call" | custom-call | flops 7247757312 | bytes 14155776 | tf_op jit(solution)/shard_map/normal/pallas_call | solution.py:121
  346.9 87.3 %all-to-all-done.1.lines_ref = bf16[16,768,384]{2,1,0:T(8,128)(2,1)} async-done(((bf16[16,768,384]{2,1,0:T(8,128)(2,1)}), bf16[16,768,384]{2,1,0:T(8,128)(2,1)}, u32[]{:S(2)}, u32[]{:S(2)}) %all-to-all-start.1) | async-done | bytes 9437216 | tf_op jit(solution)/shard_map/all_to_all | solution.py:321
  434.2 4.9 all-to-all-start.3
  441.5 21.7 %near.2 = (bf16[3,32,128,384]{3,2,1,0:T(8,128)(2,1)}, bf16[32,128,384]{2,1,0:T(8,128)(2,1)}) custom-call(f32[1]{0:T(128)S(6)} %copy.28.weight_ref, bf16[384,768]{1,0:T(8,128)(2,1)} %copy-done.3, bf16[256,256]{1,0:T(8,128)(2,1)} %fusion.1.curve_ref, bf16[256,128]{1,0:T(8,128)(2,1)} %fusion.3.cross_ref, bf16[3,32,128,384]{3,2,1,0:T(8,128)(2,1)} %base_ref.7, ...), custom_call_target="tpu_custom_call" | custom-call | flops 9059696640 | bytes 28311552 | tf_op jit(solution)/shard_map/near/pallas_call | solution.py:181
  463.2 21.7 %near.3 = (bf16[3,32,128,384]{3,2,1,0:T(8,128)(2,1)}, bf16[32,128,384]{2,1,0:T(8,128)(2,1)}) custom-call(f32[1]{0:T(128)S(6)} %copy.28.weight_ref, bf16[384,768]{1,0:T(8,128)(2,1)} %copy-done.3, bf16[256,256]{1,0:T(8,128)(2,1)} %fusion.1.curve_ref, bf16[256,128]{1,0:T(8,128)(2,1)} %fusion.3.cross_ref, ...), custom_call_target="tpu_custom_call", output_to_operand_aliasing={{0}: (8, {}), {1}: (9, {})} | custom-call | flops 9059696640 | bytes 28311552 | tf_op jit(solution)/shard_map/near/pallas_call | solution.py:181
  484.9 14.1 %normal.2 = bf16[16,4,3,32,384]{4,3,2,1,0:T(8,128)(2,1)} custom-call(bf16[512,512]{1,0:T(8,128)(2,1)} %first_ref.3, bf16[512,512]{1,0:T(8,128)(2,1)} %second_ref.3, bf16[384,384]{1,0:T(8,128)(2,1)} %maximum_maximum_fusion.stream_ref, f32[512,2]{1,0:T(8,128)} %bitcast.18, bf16[16,768,384]{2,1,0:T(8,128)(2,1)} %all-to-all-done.1.lines_ref, ...), custom_call_target="tpu_custom_call" | custom-call | flops 7247757312 | bytes 14155776 | tf_op jit(solution)/shard_map/normal/pallas_call | solution.py:121
  499.0 43.8 %all-to-all-done.3 = bf16[16,4,3,32,384]{4,3,2,1,0:T(8,128)(2,1)} async-done(((bf16[16,4,3,32,384]{4,3,2,1,0:T(8,128)(2,1)}), bf16[16,4,3,32,384]{4,3,2,1,0:T(8,128)(2,1)}, u32[]{:S(2)}, u32[]{:S(2)}) %all-to-all-start.3) | async-done | bytes 4718624 | tf_op jit(solution)/shard_map/all_to_all | solution.py:362
  542.9 4.9 all-to-all-start.2
  547.8 1.3 collective-permute-start.2
  549.1 68.2 %collective-permute-done.2.refs_0_ = bf16[32,128,384]{2,1,0:T(8,128)(2,1)S(1)} collective-permute-done((bf16[32,128,384]{2,1,0:T(8,128)(2,1)S(1)}, bf16[32,128,384]{2,1,0:T(8,128)(2,1)S(1)}, u32[]{:S(2)}, u32[]{:S(2)}) %collective-permute-start.2) | collective-permute-done | bytes 3145760 | tf_op jit(solution)/shard_map/ppermute | solution.py:354
  617.3 1.7 copy-done.1
  618.9 7.0 %finish.2.refs_1_ = bf16[3,32,128,384]{3,2,1,0:T(8,128)(2,1)} custom-call(bf16[64,3,32,384]{3,2,1,0:T(8,128)(2,1)} %bitcast.9.home_ref, bf16[3,32,128,384]{3,2,1,0:T(8,128)(2,1)} %get-tuple-element.11.refs_0_.near_ref, bf16[32,128,384]{2,1,0:T(8,128)(2,1)} %copy-done.1), custom_call_target="tpu_custom_call" | custom-call | bytes 17301504 | tf_op jit(solution)/shard_map/finish/pallas_call | solution.py:239
  625.9 25.6 %all-to-all-done.2 = bf16[16,4,3,32,384]{4,3,2,1,0:T(8,128)(2,1)} async-done(((bf16[16,4,3,32,384]{4,3,2,1,0:T(8,128)(2,1)}), bf16[16,4,3,32,384]{4,3,2,1,0:T(8,128)(2,1)}, u32[]{:S(2)}, u32[]{:S(2)}) %all-to-all-start.2) | async-done | bytes 4718624 | tf_op jit(solution)/shard_map/all_to_all | solution.py:362
  651.5 6.9 %finish.3 = bf16[3,32,128,384]{3,2,1,0:T(8,128)(2,1)} custom-call(bf16[64,3,32,384]{3,2,1,0:T(8,128)(2,1)} %bitcast.8.home_ref, bf16[3,32,128,384]{3,2,1,0:T(8,128)(2,1)} %get-tuple-element.11.refs_0_.near_ref, bf16[32,128,384]{2,1,0:T(8,128)(2,1)} %copy-done.1, bf16[3,32,128,384]{3,2,1,0:T(8,128)(2,1)} %finish.2.refs_1_), custom_call_target="tpu_custom_call", output_to_operand_aliasing={{}: (3, {})} | custom-call | bytes 17301504 | tf_op jit(solution)/shard_map/finish/pallas_call | solution.py:239
  (31 shorter events, 5.9 us)
Async XLA Ops:
  11.0 213.5 %all-to-all-start = ((bf16[16,776,384]{2,1,0:T(8,128)(2,1)}), bf16[16,776,384]{2,1,0:T(8,128)(2,1)}, u32[]{:S(2)}, u32[]{:S(2)}) async-start(bf16[16,776,384]{2,1,0:T(8,128)(2,1)} %prepare.2), calls=%async_computation | async-start | bytes 19070976 | tf_op jit(solution)/shard_map/all_to_all | solution.py:321
  26.9 103.3 %collective-permute-start = (bf16[3,16,128,384]{3,2,1,0:T(8,128)(2,1)}, bf16[3,16,128,384]{3,2,1,0:T(8,128)(2,1)S(1)}, u32[]{:S(2)}, u32[]{:S(2)}) collective-permute-start(bf16[3,16,128,384]{3,2,1,0:T(8,128)(2,1)} %get-tuple-element.14), channel_id=1, source_target_pairs={{1,0},{0,1},{3,2},{2,3},{5,4},{4,5},{7,6},{6,7},{9,8},{8,9},{11,10... | collective-permute-start | bytes 14155784 | tf_op jit(solution)/shard_map/ppermute | solution.py:295
  130.3 2.1 copy-start
  142.7 88.0 %copy-start.5 = (bf16[3,128,128]{2,1,0:T(8,128)(2,1)S(1)}, bf16[3,128,128]{2,1,0:T(8,128)(2,1)}, u32[]{:S(2)}) copy-start(bf16[3,128,128]{2,1,0:T(8,128)(2,1)} %param.15) | copy-start | bytes 294916
  224.5 209.7 %all-to-all-start.1 = ((bf16[16,768,384]{2,1,0:T(8,128)(2,1)}), bf16[16,768,384]{2,1,0:T(8,128)(2,1)}, u32[]{:S(2)}, u32[]{:S(2)}) async-start(bf16[16,768,384]{2,1,0:T(8,128)(2,1)} %prepare.3), calls=%async_computation.1 | async-start | bytes 18874368 | tf_op jit(solution)/shard_map/all_to_all | solution.py:321
  229.4 103.4 %collective-permute-start.1 = (bf16[3,16,128,384]{3,2,1,0:T(8,128)(2,1)}, bf16[3,16,128,384]{3,2,1,0:T(8,128)(2,1)}, u32[]{:S(2)}, u32[]{:S(2)}) collective-permute-start(bf16[3,16,128,384]{3,2,1,0:T(8,128)(2,1)} %get-tuple-element.13), channel_id=1, source_target_pairs={{1,0},{0,1},{3,2},{2,3},{5,4},{4,5},{7,6},{6,7},{9,8},{8,9},{11,10... | collective-permute-start | bytes 14155784 | tf_op jit(solution)/shard_map/ppermute | solution.py:295
  346.9 92.2 %copy-start.4 = (bf16[256,256]{1,0:T(8,128)(2,1)S(1)}, bf16[256,256]{1,0:T(8,128)(2,1)}, u32[]{:S(2)}) copy-start(bf16[256,256]{1,0:T(8,128)(2,1)} %param.19) | copy-start | bytes 393220
  346.9 93.2 %copy-start.6 = (bf16[3,128,128]{2,1,0:T(8,128)(2,1)S(1)}, bf16[3,128,128]{2,1,0:T(8,128)(2,1)}, u32[]{:S(2)}) copy-start(bf16[3,128,128]{2,1,0:T(8,128)(2,1)} %param.16) | copy-start | bytes 294916
  346.9 93.3 %copy-start.7 = (bf16[256,256]{1,0:T(8,128)(2,1)S(1)}, bf16[256,256]{1,0:T(8,128)(2,1)}, u32[]{:S(2)}) copy-start(bf16[256,256]{1,0:T(8,128)(2,1)} %param.20) | copy-start | bytes 393220
  434.2 108.6 %all-to-all-start.3 = ((bf16[16,4,3,32,384]{4,3,2,1,0:T(8,128)(2,1)}), bf16[16,4,3,32,384]{4,3,2,1,0:T(8,128)(2,1)}, u32[]{:S(2)}, u32[]{:S(2)}) async-start(bf16[16,4,3,32,384]{4,3,2,1,0:T(8,128)(2,1)} %normal.3), calls=%async_computation.3 | async-start | bytes 9437184 | tf_op jit(solution)/shard_map/all_to_all | solution.py:362
  440.3 1.2 copy-start.3
  499.0 48.8 %copy-start.2 = (bf16[32,128,384]{2,1,0:T(8,128)(2,1)S(1)}, bf16[32,128,384]{2,1,0:T(8,128)(2,1)}, u32[]{:S(2)}) copy-start(bf16[32,128,384]{2,1,0:T(8,128)(2,1)} %get-tuple-element.12) | copy-start | bytes 9437188
  542.9 108.6 %all-to-all-start.2 = ((bf16[16,4,3,32,384]{4,3,2,1,0:T(8,128)(2,1)}), bf16[16,4,3,32,384]{4,3,2,1,0:T(8,128)(2,1)}, u32[]{:S(2)}, u32[]{:S(2)}) async-start(bf16[16,4,3,32,384]{4,3,2,1,0:T(8,128)(2,1)} %normal.2), calls=%async_computation.2 | async-start | bytes 9437184 | tf_op jit(solution)/shard_map/all_to_all | solution.py:362
  547.8 69.5 %collective-permute-start.2 = (bf16[32,128,384]{2,1,0:T(8,128)(2,1)S(1)}, bf16[32,128,384]{2,1,0:T(8,128)(2,1)S(1)}, u32[]{:S(2)}, u32[]{:S(2)}) collective-permute-start(bf16[32,128,384]{2,1,0:T(8,128)(2,1)S(1)} %copy-done.2), channel_id=1, source_target_pairs={{0,1},{1,0},{2,3},{3,2},{4,5},{5,4},{6,7},{7,6},{8,9},{9,8},{10,11... | collective-permute-start | bytes 9437192 | tf_op jit(solution)/shard_map/ppermute | solution.py:354
  617.3 1.7 copy-start.1

commit v4 on v3

--- a/solution.py
+++ b/solution.py
@@ -314,7 +314,7 @@
                 start,
                 owners,
                 chunk,
-                16,
+                step_width(start, owners * chunk),
             )
         )
 

time: 660 us -> 659 us (level)
  transfers between devices with their start and end apart: 7 -> 7, of which waited for: 7 -> 7; matrix products, arithmetic and copies ran while one was open for 2% -> 2% of each run, Pallas kernels for 14% -> 13%
where the time goes in v4:
time: 659 us; the launch traced here: 657 us
  waiting for transfers between devices  509 us (77%)
  Pallas kernels  104 us (16%)
  starting transfers between devices  25.1 us (4%)
  local copies, waits for them, and re-layouts  14.1 us (2%)
    ppermute x2, waiting for transfers between devices, from_others(): lax.ppermute(piece, 'col', [((i + shift) % parts, i) for i in range(parts)])  202 us
    all_to_all x2, waiting for transfers between devices, per_device(): lax.all_to_all(block, 'row', 0, 0, tiled=True)  170 us
    all_to_all x2, waiting for transfers between devices, per_device(): returned.append(lax.all_to_all(term, 'row', 0, 0, tiled=True))  69.4 us
    ppermute x1, waiting for transfers between devices, per_device(): lax.ppermute(partial, 'col', [(i, (i + shift) % parts) for i in range(par...  68.2 us
    pallas_call x2, Pallas kernels, near(): pl.pallas_call(functools.partial(near_kernel, parts), grid=(count,), in_s...  43.4 us
    pallas_call x2, Pallas kernels, normal(): pl.pallas_call(normal_kernel, grid=(planes,), in_specs=[resident(operand....  28.3 us
    pallas_call x2, Pallas kernels, prepare(): pl.pallas_call(functools.partial(prepare_kernel, planes, len(profiles)),...  18.7 us
    pallas_call x2, Pallas kernels, finish(): pl.pallas_call(functools.partial(finish_kernel, len(partials)), grid=(cou...  13.9 us
  transfers between devices with their start and end apart: 7, of which 7 were waited for; matrix products, arithmetic and copies ran while one was open for 2% of the time, Pallas kernels for 13%

profile of v4, /device:TPU:11, one launch (start us, length us, event | category | flops | bytes accessed | tf_op | source)
XLA Modules:
  0.0 657.3 jit_solution(7012182027364102265)
XLA Ops:
  0.7 9.3 %prepare.2 = bf16[16,776,384]{2,1,0:T(8,128)(2,1)} custom-call(f32[1]{0:T(128)S(6)} %copy.28.weight_ref, bf16[3,32,128,384]{3,2,1,0:T(8,128)(2,1)} %base_ref.7, bf16[3,32,128,384]{3,2,1,0:T(8,128)(2,1)} %step_ref.7, bf16[3,32,128,384]{3,2,1,0:T(8,128)(2,1)} %refs_0_.5, f32[2,32]{1,0:T(2,128)} %refs_0_.3), custom_call_target="tpu_custom_call" | custom-call | bytes 23592960 | tf_op jit(solution)/shard_map/prepare/pallas_call | solution.py:69
  10.0 6.6 all-to-all-start
  16.6 9.3 %fusion.5 = (bf16[3,16,128,384]{3,2,1,0:T(8,128)(2,1)}, bf16[3,16,128,384]{3,2,1,0:T(8,128)(2,1)}) fusion(bf16[3,32,128,384]{3,2,1,0:T(8,128)(2,1)} %refs_0_.5), kind=kLoop, calls=%fused_computation.30 | loop fusion | bytes 18874368 | tf_op jit(solution)/shard_map/slice | solution.py:293
  27.1 102.1 %collective-permute-done.refs_0_.refs_1_ = bf16[3,16,128,384]{3,2,1,0:T(8,128)(2,1)S(1)} collective-permute-done((bf16[3,16,128,384]{3,2,1,0:T(8,128)(2,1)}, bf16[3,16,128,384]{3,2,1,0:T(8,128)(2,1)S(1)}, u32[]{:S(2)}, u32[]{:S(2)}) %collective-permute-start) | collective-permute-done | bytes 4718624 | tf_op jit(solution)/shard_map/ppermute | solution.py:295
  129.2 2.1 copy-done
  131.3 9.3 %prepare.3 = bf16[16,768,384]{2,1,0:T(8,128)(2,1)} custom-call(f32[1]{0:T(128)S(6)} %copy.28.weight_ref, bf16[3,32,128,384]{3,2,1,0:T(8,128)(2,1)} %base_ref.7, bf16[3,32,128,384]{3,2,1,0:T(8,128)(2,1)} %step_ref.7, bf16[3,32,128,384]{3,2,1,0:T(8,128)(2,1)} %refs_0_.5, bf16[3,16,128,384]{3,2,1,0:T(8,128)(2,1)} %copy-done), custom_call_target="tpu_custom_call" | custom-call | bytes 23592960 | tf_op jit(solution)/shard_map/prepare/pallas_call | solution.py:69
  140.7 82.8 %all-to-all-done.lines_ref = bf16[16,776,384]{2,1,0:T(8,128)(2,1)} async-done(((bf16[16,776,384]{2,1,0:T(8,128)(2,1)}), bf16[16,776,384]{2,1,0:T(8,128)(2,1)}, u32[]{:S(2)}, u32[]{:S(2)}) %all-to-all-start) | async-done | bytes 9535520 | tf_op jit(solution)/shard_map/all_to_all | solution.py:321
  223.5 4.9 all-to-all-start.1
  228.4 1.2 collective-permute-start.1
  232.1 99.7 %collective-permute-done.1.refs_1_.refs_0_ = bf16[3,16,128,384]{3,2,1,0:T(8,128)(2,1)} collective-permute-done((bf16[3,16,128,384]{3,2,1,0:T(8,128)(2,1)}, bf16[3,16,128,384]{3,2,1,0:T(8,128)(2,1)}, u32[]{:S(2)}, u32[]{:S(2)}) %collective-permute-start.1) | collective-permute-done | bytes 4718624 | tf_op jit(solution)/shard_map/ppermute | solution.py:295
  331.7 14.1 %normal.3 = bf16[16,4,3,32,384]{4,3,2,1,0:T(8,128)(2,1)} custom-call(bf16[512,512]{1,0:T(8,128)(2,1)} %first_ref.3, bf16[512,512]{1,0:T(8,128)(2,1)} %second_ref.3, bf16[384,384]{1,0:T(8,128)(2,1)} %maximum_maximum_fusion.stream_ref, f32[512,2]{1,0:T(8,128)} %bitcast.17, bf16[16,776,384]{2,1,0:T(8,128)(2,1)} %all-to-all-done.lines_ref, ...), custom_call_target="tpu_custom_call" | custom-call | flops 7247757312 | bytes 14155776 | tf_op jit(solution)/shard_map/normal/pallas_call | solution.py:121
  345.9 87.3 %all-to-all-done.1.lines_ref = bf16[16,768,384]{2,1,0:T(8,128)(2,1)} async-done(((bf16[16,768,384]{2,1,0:T(8,128)(2,1)}), bf16[16,768,384]{2,1,0:T(8,128)(2,1)}, u32[]{:S(2)}, u32[]{:S(2)}) %all-to-all-start.1) | async-done | bytes 9437216 | tf_op jit(solution)/shard_map/all_to_all | solution.py:321
  433.2 4.9 all-to-all-start.3
  440.4 21.7 %near.2 = (bf16[3,32,128,384]{3,2,1,0:T(8,128)(2,1)}, bf16[32,128,384]{2,1,0:T(8,128)(2,1)}) custom-call(f32[1]{0:T(128)S(6)} %copy.28.weight_ref, bf16[384,768]{1,0:T(8,128)(2,1)} %copy-done.3, bf16[256,256]{1,0:T(8,128)(2,1)} %fusion.1.curve_ref, bf16[256,128]{1,0:T(8,128)(2,1)} %fusion.3.cross_ref, bf16[3,32,128,384]{3,2,1,0:T(8,128)(2,1)} %base_ref.7, ...), custom_call_target="tpu_custom_call" | custom-call | flops 9059696640 | bytes 28311552 | tf_op jit(solution)/shard_map/near/pallas_call | solution.py:181
  462.2 21.7 %near.3 = (bf16[3,32,128,384]{3,2,1,0:T(8,128)(2,1)}, bf16[32,128,384]{2,1,0:T(8,128)(2,1)}) custom-call(f32[1]{0:T(128)S(6)} %copy.28.weight_ref, bf16[384,768]{1,0:T(8,128)(2,1)} %copy-done.3, bf16[256,256]{1,0:T(8,128)(2,1)} %fusion.1.curve_ref, bf16[256,128]{1,0:T(8,128)(2,1)} %fusion.3.cross_ref, ...), custom_call_target="tpu_custom_call", output_to_operand_aliasing={{0}: (8, {}), {1}: (9, {})} | custom-call | flops 9059696640 | bytes 28311552 | tf_op jit(solution)/shard_map/near/pallas_call | solution.py:181
  483.9 14.1 %normal.2 = bf16[16,4,3,32,384]{4,3,2,1,0:T(8,128)(2,1)} custom-call(bf16[512,512]{1,0:T(8,128)(2,1)} %first_ref.3, bf16[512,512]{1,0:T(8,128)(2,1)} %second_ref.3, bf16[384,384]{1,0:T(8,128)(2,1)} %maximum_maximum_fusion.stream_ref, f32[512,2]{1,0:T(8,128)} %bitcast.18, bf16[16,768,384]{2,1,0:T(8,128)(2,1)} %all-to-all-done.1.lines_ref, ...), custom_call_target="tpu_custom_call" | custom-call | flops 7247757312 | bytes 14155776 | tf_op jit(solution)/shard_map/normal/pallas_call | solution.py:121
  498.0 43.8 %all-to-all-done.3 = bf16[16,4,3,32,384]{4,3,2,1,0:T(8,128)(2,1)} async-done(((bf16[16,4,3,32,384]{4,3,2,1,0:T(8,128)(2,1)}), bf16[16,4,3,32,384]{4,3,2,1,0:T(8,128)(2,1)}, u32[]{:S(2)}, u32[]{:S(2)}) %all-to-all-start.3) | async-done | bytes 4718624 | tf_op jit(solution)/shard_map/all_to_all | solution.py:362
  541.8 4.9 all-to-all-start.2
  546.7 1.3 collective-permute-start.2
  548.0 68.2 %collective-permute-done.2.refs_0_ = bf16[32,128,384]{2,1,0:T(8,128)(2,1)S(1)} collective-permute-done((bf16[32,128,384]{2,1,0:T(8,128)(2,1)S(1)}, bf16[32,128,384]{2,1,0:T(8,128)(2,1)S(1)}, u32[]{:S(2)}, u32[]{:S(2)}) %collective-permute-start.2) | collective-permute-done | bytes 3145760 | tf_op jit(solution)/shard_map/ppermute | solution.py:354
  616.2 1.7 copy-done.1
  617.9 7.0 %finish.2.refs_1_ = bf16[3,32,128,384]{3,2,1,0:T(8,128)(2,1)} custom-call(bf16[64,3,32,384]{3,2,1,0:T(8,128)(2,1)} %bitcast.9.home_ref, bf16[3,32,128,384]{3,2,1,0:T(8,128)(2,1)} %get-tuple-element.11.refs_0_.near_ref, bf16[32,128,384]{2,1,0:T(8,128)(2,1)} %copy-done.1), custom_call_target="tpu_custom_call" | custom-call | bytes 17301504 | tf_op jit(solution)/shard_map/finish/pallas_call | solution.py:239
  624.9 25.6 %all-to-all-done.2 = bf16[16,4,3,32,384]{4,3,2,1,0:T(8,128)(2,1)} async-done(((bf16[16,4,3,32,384]{4,3,2,1,0:T(8,128)(2,1)}), bf16[16,4,3,32,384]{4,3,2,1,0:T(8,128)(2,1)}, u32[]{:S(2)}, u32[]{:S(2)}) %all-to-all-start.2) | async-done | bytes 4718624 | tf_op jit(solution)/shard_map/all_to_all | solution.py:362
  650.4 6.9 %finish.3 = bf16[3,32,128,384]{3,2,1,0:T(8,128)(2,1)} custom-call(bf16[64,3,32,384]{3,2,1,0:T(8,128)(2,1)} %bitcast.8.home_ref, bf16[3,32,128,384]{3,2,1,0:T(8,128)(2,1)} %get-tuple-element.11.refs_0_.near_ref, bf16[32,128,384]{2,1,0:T(8,128)(2,1)} %copy-done.1, bf16[3,32,128,384]{3,2,1,0:T(8,128)(2,1)} %finish.2.refs_1_), custom_call_target="tpu_custom_call", output_to_operand_aliasing={{}: (3, {})} | custom-call | bytes 17301504 | tf_op jit(solution)/shard_map/finish/pallas_call | solution.py:239
  (31 shorter events, 5.9 us)
Async XLA Ops:
  10.0 213.5 %all-to-all-start = ((bf16[16,776,384]{2,1,0:T(8,128)(2,1)}), bf16[16,776,384]{2,1,0:T(8,128)(2,1)}, u32[]{:S(2)}, u32[]{:S(2)}) async-start(bf16[16,776,384]{2,1,0:T(8,128)(2,1)} %prepare.2), calls=%async_computation | async-start | bytes 19070976 | tf_op jit(solution)/shard_map/all_to_all | solution.py:321
  25.9 103.3 %collective-permute-start = (bf16[3,16,128,384]{3,2,1,0:T(8,128)(2,1)}, bf16[3,16,128,384]{3,2,1,0:T(8,128)(2,1)S(1)}, u32[]{:S(2)}, u32[]{:S(2)}) collective-permute-start(bf16[3,16,128,384]{3,2,1,0:T(8,128)(2,1)} %get-tuple-element.14), channel_id=1, source_target_pairs={{1,0},{0,1},{3,2},{2,3},{5,4},{4,5},{7,6},{6,7},{9,8},{8,9},{11,10... | collective-permute-start | bytes 14155784 | tf_op jit(solution)/shard_map/ppermute | solution.py:295
  129.2 2.1 copy-start
  140.7 89.0 %copy-start.5 = (bf16[3,128,128]{2,1,0:T(8,128)(2,1)S(1)}, bf16[3,128,128]{2,1,0:T(8,128)(2,1)}, u32[]{:S(2)}) copy-start(bf16[3,128,128]{2,1,0:T(8,128)(2,1)} %param.15) | copy-start | bytes 294916
  223.5 209.7 %all-to-all-start.1 = ((bf16[16,768,384]{2,1,0:T(8,128)(2,1)}), bf16[16,768,384]{2,1,0:T(8,128)(2,1)}, u32[]{:S(2)}, u32[]{:S(2)}) async-start(bf16[16,768,384]{2,1,0:T(8,128)(2,1)} %prepare.3), calls=%async_computation.1 | async-start | bytes 18874368 | tf_op jit(solution)/shard_map/all_to_all | solution.py:321
  228.4 103.4 %collective-permute-start.1 = (bf16[3,16,128,384]{3,2,1,0:T(8,128)(2,1)}, bf16[3,16,128,384]{3,2,1,0:T(8,128)(2,1)}, u32[]{:S(2)}, u32[]{:S(2)}) collective-permute-start(bf16[3,16,128,384]{3,2,1,0:T(8,128)(2,1)} %get-tuple-element.13), channel_id=1, source_target_pairs={{1,0},{0,1},{3,2},{2,3},{5,4},{4,5},{7,6},{6,7},{9,8},{8,9},{11,10... | collective-permute-start | bytes 14155784 | tf_op jit(solution)/shard_map/ppermute | solution.py:295
  345.9 92.2 %copy-start.4 = (bf16[256,256]{1,0:T(8,128)(2,1)S(1)}, bf16[256,256]{1,0:T(8,128)(2,1)}, u32[]{:S(2)}) copy-start(bf16[256,256]{1,0:T(8,128)(2,1)} %param.19) | copy-start | bytes 393220
  345.9 93.2 %copy-start.6 = (bf16[3,128,128]{2,1,0:T(8,128)(2,1)S(1)}, bf16[3,128,128]{2,1,0:T(8,128)(2,1)}, u32[]{:S(2)}) copy-start(bf16[3,128,128]{2,1,0:T(8,128)(2,1)} %param.16) | copy-start | bytes 294916
  345.9 93.4 %copy-start.7 = (bf16[256,256]{1,0:T(8,128)(2,1)S(1)}, bf16[256,256]{1,0:T(8,128)(2,1)}, u32[]{:S(2)}) copy-start(bf16[256,256]{1,0:T(8,128)(2,1)} %param.20) | copy-start | bytes 393220
  433.2 108.6 %all-to-all-start.3 = ((bf16[16,4,3,32,384]{4,3,2,1,0:T(8,128)(2,1)}), bf16[16,4,3,32,384]{4,3,2,1,0:T(8,128)(2,1)}, u32[]{:S(2)}, u32[]{:S(2)}) async-start(bf16[16,4,3,32,384]{4,3,2,1,0:T(8,128)(2,1)} %normal.3), calls=%async_computation.3 | async-start | bytes 9437184 | tf_op jit(solution)/shard_map/all_to_all | solution.py:362
  439.2 1.2 copy-start.3
  498.0 48.7 %copy-start.2 = (bf16[32,128,384]{2,1,0:T(8,128)(2,1)S(1)}, bf16[32,128,384]{2,1,0:T(8,128)(2,1)}, u32[]{:S(2)}) copy-start(bf16[32,128,384]{2,1,0:T(8,128)(2,1)} %get-tuple-element.12) | copy-start | bytes 9437188
  541.8 108.6 %all-to-all-start.2 = ((bf16[16,4,3,32,384]{4,3,2,1,0:T(8,128)(2,1)}), bf16[16,4,3,32,384]{4,3,2,1,0:T(8,128)(2,1)}, u32[]{:S(2)}, u32[]{:S(2)}) async-start(bf16[16,4,3,32,384]{4,3,2,1,0:T(8,128)(2,1)} %normal.2), calls=%async_computation.2 | async-start | bytes 9437184 | tf_op jit(solution)/shard_map/all_to_all | solution.py:362
  546.7 69.5 %collective-permute-start.2 = (bf16[32,128,384]{2,1,0:T(8,128)(2,1)S(1)}, bf16[32,128,384]{2,1,0:T(8,128)(2,1)S(1)}, u32[]{:S(2)}, u32[]{:S(2)}) collective-permute-start(bf16[32,128,384]{2,1,0:T(8,128)(2,1)S(1)} %copy-done.2), channel_id=1, source_target_pairs={{0,1},{1,0},{2,3},{3,2},{4,5},{5,4},{6,7},{7,6},{8,9},{9,8},{10,11... | collective-permute-start | bytes 9437192 | tf_op jit(solution)/shard_map/ppermute | solution.py:354
  616.2 1.7 copy-start.1
